TPU v7x, 32 devices: a whole 2x2x4 slice. The times are simulated.
32 devices in a mesh: rep: 8 (over z, x), shard: 4 (over y, core).
Axes of the slice: x: 2, y: 2, z: 4, core: 2. Of those that a mesh axis runs over, the one named last changes fastest.
Arguments:
- tokens: bfloat16 [16384, 1024], P(('rep', 'shard')), may hold values from -6 to 6
- positions: int32 [16384], P(('rep', 'shard')), may hold values from 0 to 511, as said below
- lengths: int32 [64], replicated, may hold values from 0 to 512, as said below
- owner: int32 [64], replicated, may hold values from 0 to 31, as said below
- qkv_weight: bfloat16 [1024, 3072], P('shard'), may hold values from -0.1875 to 0.1875
- out_weight: bfloat16 [1024, 1024], P('shard'), may hold values from -1.5 to 1.5
- in_weight: bfloat16 [1024, 4096], P('shard'), may hold values from -0.1875 to 0.1875
- in_bias: bfloat16 [4096], P('shard'), may hold values from -3 to 3
- fc_weight: bfloat16 [4096, 1024], P('shard'), may hold values from -0.09375 to 0.09375
- fc_bias: bfloat16 [1024], P('shard'), may hold values from -3 to 3
- norm_gain: bfloat16 [1024], P('shard'), may hold values from 0.25 to 1.75
- norm_bias: bfloat16 [1024], P('shard'), may hold values from -2 to 2
- cotangent: bfloat16 [16384, 1024], P(('rep', 'shard')), may hold values from -6 to 6
Outputs:
- layer_out: bfloat16 [16384, 1024], P(('rep', 'shard'))
- input_grad: bfloat16 [16384, 1024], P(('rep', 'shard'))
- grad_qkv: float32 [1024, 3072], P('shard')
- grad_out: float32 [1024, 1024], P('shard')
- grad_in: float32 [1024, 4096], P('shard')
- grad_in_bias: float32 [4096], P('shard')
- grad_fc: float32 [4096, 1024], P('shard')
- grad_fc_bias: float32 [1024], P('shard')
- grad_gain: float32 [1024], P('shard')
- grad_norm_bias: float32 [1024], P('shard')
Inputs may be any that keep to these rules, and one draw needn't show every extreme that they name: Sequences 2 i and 2 i + 1 go to one device; their lengths sum to at most 512; some sequence has exactly 512 tokens; a length may be 0. Sequences 2 i and 2 i + 1 have the same owner, and every device owns exactly one such pair. `positions`: a token's position within its sequence, with the sequences packed as the steps say; unused slots hold 0.
All inputs are finite; a program needn't handle non-finite values.
Results may differ from a plain program's by a relative error of at most 0.011.
Values may be sent and summed in bfloat16 or wider, within the bound.
A program may use at most 256 MiB of HBM per device.

v0:
```python
import functools
from functools import partial
import math

import jax
import jax.numpy as jnp
from jax import lax
from jax.experimental import pallas as pl
from jax.experimental.pallas import tpu as pltpu
from jax.sharding import PartitionSpec as P

D = 1024
HEADS = 16
HEAD_DIM = 64
ROT_DIM = 32
TOK_DEV = 512

MESH = pl.DeviceIdType.MESH
BLK = 128
COL = 512
SLOTS = 8
LAGS = (1, 2, 2, 2, 2, 2, 2, 2)

EPS = 1e-05
NEG = -1000000000.0
GELU_C = math.sqrt(2.0 / math.pi)
GELU_A = 0.044715
GATHER_LAGS = (0, 2, 4, 5)
SCORE_SCALE = 0.125


def layout(lengths, owner, device):
    owned_mask = (owner == device).astype(jnp.int32)
    seq_ends = jnp.cumsum(lengths * owned_mask)
    seq_load = jnp.sum(lengths * owned_mask)
    slot_index = jnp.arange(TOK_DEV, dtype=jnp.int32)
    passed = (seq_ends[None, :] <= slot_index[:, None]) & (owned_mask[None, :] > 0)
    segment = jnp.sum(passed.astype(jnp.int32), axis=1)
    in_use = slot_index < seq_load
    return (jnp.where(in_use, segment, TOK_DEV + slot_index), in_use)


def layer_norm(inputs, scale_gain, norm_shift):
    center = inputs - jnp.mean(inputs, axis=-1, keepdims=True)
    spread = jnp.mean(center * center, axis=-1, keepdims=True)
    return center * lax.rsqrt(spread + EPS) * scale_gain + norm_shift


def rotary_tables(positions):
    lane = jnp.arange(128, dtype=jnp.int32) % HEAD_DIM
    rotated = lane < ROT_DIM
    inverse = jnp.exp((lane // 2).astype(jnp.float32) * (-2.0 * math.log(10000.0) / ROT_DIM))
    angles = positions.astype(jnp.float32)[:, None] * jnp.where(rotated, inverse, 0.0)[None, :]
    sine = jnp.sin(angles)
    even = (lane % 2 == 0)[None, :]
    return (jnp.cos(angles), jnp.where(even, -sine, 0.0), jnp.where(even, 0.0, sine))


GATHER_CHUNKS = (4, 4, 4, 1)
FBLK = 256


def front_kernel(tok_ref, up_ref, cos_ref, sa_ref, sb_ref, small_ref, in_own, fc_own, qkv_own, out_own,
                 normed_ref, active_ref, gh_ref, rows_ref, base_ref, gn_ref, ga_ref, gib_ref, norm_ref,
                 qkv_full, out_full,
                 in_full, fc_full, small_full, bias_ref,
                 send_sem, recv_sem, core_send, core_recv, own_send, own_recv, local_sem, s_send, s_recv):
    rep = lax.axis_index("rep")
    shard = lax.axis_index("shard")
    y, c = shard // 2, shard % 2
    b0, b1 = rep % 2, (rep // 2) % 2
    core_shard = 2 * y + 1 - c
    other = 2 * (1 - y) + c
    diagonal = 2 * (1 - y) + 1 - c
    core_peer = (rep, core_shard)
    y_peer = (rep, other)
    diagonal_peer = (rep, diagonal)
    peer0 = (rep + 1 - 2 * b0, shard)
    peer1 = (rep + 2 - 4 * b1, shard)
    group = (core_peer, y_peer, diagonal_peer)

    barrier = pltpu.get_barrier_semaphore()
    for p in group + (peer0, peer1):
        pl.semaphore_signal(barrier, inc=1, device_id=p, device_id_type=MESH)
    pl.semaphore_wait(barrier, 5)

    owns = (in_own, fc_own, qkv_own, out_own)
    fulls = (in_full, fc_full, qkv_full, out_full)
    chunks = [(a, k) for a in range(4) for k in range(GATHER_CHUNKS[a])]
    n = len(chunks)
    ways = ((b0 + 2 * b1, b1, peer0, peer1), (b1 + 2 * b0, b0, peer1, peer0))

    def remote(src, dst, sems, index, peer):
        return pltpu.make_async_remote_copy(
            src_ref=src, dst_ref=dst, send_sem=sems[0].at[index], recv_sem=sems[1].at[index],
            device_id=peer, device_id_type=MESH)

    def place(i, h):
        a, k = chunks[i]
        own, full = owns[a], fulls[a]
        rows, cols = own.shape
        piece = rows // GATHER_CHUNKS[a] // 4
        return own, full, rows, k * 4 * piece, piece, pl.ds(h * (cols // 2), cols // 2)

    def y_copy(i, h):
        own, full, rows, start, piece, cols = place(i, h)
        at = pl.multiple_of(start + ways[h][0] * piece, 16)
        return remote(own.at[pl.ds(at, piece), cols],
                      full.at[pl.ds(pl.multiple_of(shard * rows + at, 16), piece), cols],
                      (send_sem, recv_sem), (0, i, h), y_peer)

    def first_copy(i, h):
        own, full, rows, start, piece, cols = place(i, h)
        at = pl.multiple_of(other * rows + start + ways[h][0] * piece, 16)
        ref = full.at[pl.ds(at, piece), cols]
        return remote(ref, ref, (send_sem, recv_sem), (1, i, h), ways[h][2])

    def second_copy(i, h):
        own, full, rows, start, piece, cols = place(i, h)
        at = pl.multiple_of(other * rows + start + ways[h][1] * 2 * piece, 16)
        ref = full.at[pl.ds(at, 2 * piece), cols]
        return remote(ref, ref, (send_sem, recv_sem), (2, i, h), ways[h][3])

    def core_copy(i):
        own, full, rows, start, piece, cols = place(i, 0)
        ref = full.at[pl.ds(pl.multiple_of(other * rows + start, 16), 4 * piece)]
        return remote(ref, ref, (core_send, core_recv), (i,), core_peer)

    def own_rows(a):
        rows = owns[a].shape[0]
        return fulls[a].at[pl.ds(pl.multiple_of(shard * rows, 16), rows)]

    def own_copy(a):
        return remote(owns[a], own_rows(a), (own_send, own_recv), (a,), core_peer)

    def local_copy(a):
        return pltpu.make_async_copy(owns[a], own_rows(a), local_sem.at[a])

    def small_copy(j):
        return remote(small_ref, small_full.at[shard], (s_send, s_recv), (j,), group[j])

    for j in range(3):
        small_copy(j).start()
    for i in range(n):
        for h in range(2):
            y_copy(i, h).start()
    for a in range(4):
        own_copy(a).start()
        local_copy(a).start()

    def norm_all():
        small_full[shard] = small_ref[...]
        for j in range(3):
            small_copy(j).wait()
        for o in range(4):
            for r in range(8):
                bias_ref[0:1, (o * 8 + r) * 128:(o * 8 + r + 1) * 128] = small_full[o, r:r + 1, :]
            for r in range(2):
                span = slice((o * 2 + r) * 128, (o * 2 + r + 1) * 128)
                norm_ref[2:3, span] = small_full[o, 8 + r:9 + r, :]
                norm_ref[0:1, span] = small_full[o, 10 + r:11 + r, :]
                norm_ref[1:2, span] = small_full[o, 12 + r:13 + r, :]

        def rows_step(r, carry):
            at = pl.ds(pl.multiple_of(r * 64, 64), 64)
            x = tok_ref[at, :].astype(jnp.float32)
            center = x - jnp.mean(x, axis=-1, keepdims=True)
            spread = jnp.mean(center * center, axis=-1, keepdims=True)
            normed = center * lax.rsqrt(spread + EPS) * norm_ref[0:1, :] + norm_ref[1:2, :]
            normed_ref[at, :] = normed.astype(jnp.bfloat16)
            base_ref[at, :] = x + norm_ref[2:3, :]
            return carry
        lax.fori_loop(0, TOK_DEV // 64, rows_step, 0)

    def span(j):
        return pl.ds(pl.multiple_of(j * FBLK, FBLK), FBLK)

    def hidden_block(j, carry):
        at = span(j)
        hidden = jnp.dot(normed_ref[...], in_full[:, at], preferred_element_type=jnp.float32) + bias_ref[0:1, at]
        cube = hidden * hidden
        turn = jnp.tanh(GELU_C * hidden * (1.0 + GELU_A * cube))
        half = 0.5 * (1.0 + turn)
        active_ref[:, at] = (hidden * half).astype(jnp.bfloat16)
        slope = half + 0.5 * hidden * (1.0 - turn * turn) * (GELU_C * (1.0 + 3.0 * GELU_A * cube))
        gh_ref[:, at] = slope.astype(jnp.bfloat16)
        return carry

    def back_block(j, carry):
        at = span(j)
        grad = lax.dot_general(up_ref[...], fc_full[at, :], (((1,), (1,)), ((), ())), preferred_element_type=jnp.float32)
        low = (grad * gh_ref[:, at].astype(jnp.float32)).astype(jnp.bfloat16)
        gh_ref[:, at] = low
        gib_ref[0:1, at] = jnp.sum(low.astype(jnp.float32), axis=0, keepdims=True)
        return carry

    def mlp_block(j, carry):
        at = span(j)
        base_ref[:, at] = base_ref[:, at] + jnp.dot(active_ref[...], fc_full[:, at], preferred_element_type=jnp.float32)
        gn_ref[:, at] = lax.dot_general(gh_ref[...], in_full[at, :], (((1,), (1,)), ((), ())), preferred_element_type=jnp.float32)
        return carry

    def turn_block(j, carry):
        at = span(j)
        rows = jnp.dot(normed_ref[...], qkv_full[:, at], preferred_element_type=jnp.float32)
        for g in range(FBLK // 128):
            part = rows[:, g * 128:(g + 1) * 128]
            turned = part * cos_ref[...] + pltpu.roll(part, 127, 1) * sa_ref[...] + pltpu.roll(part, 1, 1) * sb_ref[...]
            rows_ref[:, pl.ds(pl.multiple_of(j * FBLK + g * 128, 128), 128)] = turned.astype(jnp.bfloat16)
        return carry

    def value_block(j, carry):
        at = span(j)
        rows_ref[:, at] = jnp.dot(normed_ref[...], qkv_full[:, at], preferred_element_type=jnp.float32).astype(jnp.bfloat16)
        return carry

    def out_block(j, carry):
        at = span(j)
        ga_ref[:, at] = lax.dot_general(up_ref[...], out_full[at, :], (((1,), (1,)), ((), ())), preferred_element_type=jnp.float32).astype(jnp.bfloat16)
        return carry

    def loop(block, lo, hi):
        lax.fori_loop(lo, hi, block, 0)

    work = {0: [norm_all]}
    nf = 4096 // FBLK
    lag = GATHER_LAGS
    ends = [sum(GATHER_CHUNKS[:a + 1]) - 1 + lag[3] for a in range(4)]

    def ready(a):
        own_copy(a).wait_recv()
        local_copy(a).wait()

    def plan(step, *todo):
        work.setdefault(step, []).extend(todo)

    plan(ends[0], functools.partial(ready, 0))
    for j in range(4):
        plan(ends[0] + j, functools.partial(loop, hidden_block, j * nf // 4, (j + 1) * nf // 4))
    plan(ends[1], functools.partial(ready, 1))
    for j in range(4):
        plan(ends[1] + j, functools.partial(loop, back_block, j * nf // 4, (j + 1) * nf // 4))
    plan(ends[2], functools.partial(ready, 2), functools.partial(loop, mlp_block, 0, D // FBLK),
         functools.partial(loop, turn_block, 0, 2 * D // FBLK), functools.partial(loop, value_block, 2 * D // FBLK, 3 * D // FBLK))
    plan(ends[3], functools.partial(ready, 3), functools.partial(loop, out_block, 0, D // FBLK))

    for i in range(n + lag[3]):
        if i < n:
            for h in range(2):
                y_copy(i, h).wait_recv()
                first_copy(i, h).start()
        if 0 <= i - lag[1] < n:
            for h in range(2):
                first_copy(i - lag[1], h).wait_recv()
                second_copy(i - lag[1], h).start()
        if 0 <= i - lag[2] < n:
            for h in range(2):
                second_copy(i - lag[2], h).wait_recv()
            core_copy(i - lag[2]).start()
        if 0 <= i - lag[3] < n:
            core_copy(i - lag[3]).wait_recv()
        for todo in work.get(i, []):
            todo()
    for i in range(n):
        for h in range(2):
            y_copy(i, h).wait_send()
            first_copy(i, h).wait_send()
            second_copy(i, h).wait_send()
        core_copy(i).wait_send()
    for a in range(4):
        own_copy(a).wait_send()


def front(tokens, upstream, tables, small, in_own, fc_own, qkv_own, out_own, shards):
    bf, f32 = jnp.bfloat16, jnp.float32
    rows = tokens.shape[0]
    ff = in_own.shape[1]
    n = sum(GATHER_CHUNKS)
    vm = pl.BlockSpec(memory_space=pltpu.VMEM)
    hbm = pl.BlockSpec(memory_space=pl.ANY)

    def full(own):
        return (own.shape[0] * shards, own.shape[1])
    out_shape = [
        ((rows, D), bf), ((rows, ff), bf), ((rows, ff), bf), ((rows, 3 * D), bf), ((rows, D), f32), ((rows, D), f32),
        ((rows, D), bf), ((1, ff), f32), ((8, D), f32), (full(qkv_own), bf), (full(out_own), bf),
    ]
    dma = pltpu.SemaphoreType.DMA
    return pl.pallas_call(
        front_kernel,
        out_shape=[jax.ShapeDtypeStruct(s, d) for s, d in out_shape],
        in_specs=[vm] * 6 + [hbm] * 4,
        out_specs=[vm] * len(out_shape),
        scratch_shapes=[
            pltpu.VMEM(full(in_own), bf), pltpu.VMEM(full(fc_own), bf),
            pltpu.VMEM((shards,) + small.shape, f32), pltpu.VMEM((1, ff), f32),
            dma((3, n, 2)), dma((3, n, 2)), dma((n,)), dma((n,)), dma((4,)), dma((4,)), dma((4,)), dma((3,)), dma((3,)),
        ],
        compiler_params=pltpu.CompilerParams(collective_id=2, has_side_effects=True, vmem_limit_bytes=62 * 2**20),
        name="front",
    )(tokens, upstream, *tables, small, in_own, fc_own, qkv_own, out_own)


def attention_kernel(q_ref, k_ref, v_ref, ga_ref, seg_col, seg_row, cos_ref, sa_ref, sb_ref, att_ref, gm_ref, bias_ref):
    pair = pl.program_id(0)

    @pl.when(pair == 0)
    def _():
        row = lax.broadcasted_iota(jnp.int32, (TOK_DEV, TOK_DEV), 0)
        col = lax.broadcasted_iota(jnp.int32, (TOK_DEV, TOK_DEV), 1)
        allowed = (seg_col[...] == seg_row[...]) & (col <= row)
        bias_ref[...] = jnp.where(allowed, 0.0, NEG)

    attend_pair(pair, q_ref[...], k_ref[...], v_ref[...], ga_ref[...], bias_ref, cos_ref, sa_ref, sb_ref,
                lambda value: att_ref.__setitem__(Ellipsis, value),
                lambda part, value: gm_ref.__setitem__((slice(None), pl.ds(pl.multiple_of(part * D + pair * 128, 128), 128)), value))


QBLK = 256


def attend_pair(pair, q, k, v, ga, bias_ref, cos_ref, sa_ref, sb_ref, put_att, put_grad):
    f32, bf = jnp.float32, jnp.bfloat16
    nt = (((1,), (1,)), ((), ()))
    tn = (((0,), (0,)), ((), ()))
    lane = lax.broadcasted_iota(jnp.int32, (1, 128), 1)
    keep = [(lane < HEAD_DIM).astype(f32).astype(bf), (lane >= HEAD_DIM).astype(f32).astype(bf)]
    q = q * jnp.asarray(SCORE_SCALE, bf)
    attended, grad_q = [], []
    grad_k, grad_v = {}, {}
    n_blocks = TOK_DEV // QBLK

    def add(store, block, value):
        store[block] = value if block not in store else store[block] + value

    for r in range(n_blocks):
        rows = slice(r * QBLK, (r + 1) * QBLK)
        keys = (r + 1) * QBLK
        att = gq = None
        for h in range(2):
            qh = q[rows] * keep[h]
            gh = ga[rows] * keep[h]
            kh = k[:keys] * keep[h]
            vh = v[:keys] * keep[h]
            scores = lax.dot_general(qh, k[:keys], nt, preferred_element_type=f32) + bias_ref[rows, :keys]
            weight = jnp.exp(scores - jnp.max(scores, axis=-1, keepdims=True))
            soft = weight * (1.0 / jnp.sum(weight, axis=-1, keepdims=True))
            low = soft.astype(bf)
            grad_soft = lax.dot_general(gh, v[:keys], nt, preferred_element_type=f32)
            weighted = soft * grad_soft
            delta = jnp.sum(weighted, axis=-1, keepdims=True)
            grad_scores = (weighted - soft * delta).astype(bf)
            part = jnp.dot(low, vh, preferred_element_type=f32)
            att = part if att is None else att + part
            part = jnp.dot(grad_scores, kh, preferred_element_type=f32)
            gq = part if gq is None else gq + part
            gk = lax.dot_general(grad_scores, qh, tn, preferred_element_type=f32)
            gv = lax.dot_general(low, gh, tn, preferred_element_type=f32)
            for b in range(r + 1):
                span = slice(b * QBLK, (b + 1) * QBLK)
                add(grad_k, b, gk[span])
                add(grad_v, b, gv[span])
        attended.append(att)
        grad_q.append(gq)

    def unturn(x):
        x = x.astype(bf).astype(f32)
        return x * cos_ref[...] - pltpu.roll(x, 127, 1) * sa_ref[...] - pltpu.roll(x, 1, 1) * sb_ref[...]

    put_att(jnp.concatenate(attended, 0).astype(bf))
    put_grad(0, unturn(jnp.concatenate(grad_q, 0) * SCORE_SCALE).astype(bf))
    put_grad(1, unturn(jnp.concatenate([grad_k[b] for b in range(n_blocks)], 0)).astype(bf))
    put_grad(2, jnp.concatenate([grad_v[b] for b in range(n_blocks)], 0).astype(bf))


def attention(rows, ga, segment, tables):
    bf = jnp.bfloat16
    t = rows.shape[0]
    pairs = HEADS // 2
    whole = pl.BlockSpec(memory_space=pltpu.VMEM)
    return pl.pallas_call(
        attention_kernel,
        grid=(pairs,),
        out_shape=[jax.ShapeDtypeStruct((t, D), bf), jax.ShapeDtypeStruct((t, 3 * D), bf)],
        in_specs=[
            pl.BlockSpec((t, 128), lambda p: (0, p)), pl.BlockSpec((t, 128), lambda p: (0, pairs + p)),
            pl.BlockSpec((t, 128), lambda p: (0, 2 * pairs + p)), pl.BlockSpec((t, 128), lambda p: (0, p)),
            whole, whole, whole, whole, whole,
        ],
        out_specs=[pl.BlockSpec((t, 128), lambda p: (0, p)), pl.BlockSpec((t, 3 * D), lambda p: (0, 0))],
        scratch_shapes=[pltpu.VMEM((t, t), jnp.float32)],
        compiler_params=pltpu.CompilerParams(vmem_limit_bytes=48 * 2**20),
        name="attention",
    )(rows, rows, rows, ga, segment[:, None], segment[None, :], *tables)


def reduce_kernel(n_rep, normed_hbm, attended_hbm, active_hbm, gm_hbm, up_hbm, gh_hbm, small_ref, out_ref, small_out,
                  left, right, turned, load_sem, c_send, c_keep, c_recv, y_send, y_keep, y_recv, work, recvs, s_buf, s_recv,
                  send_sem, recv_sem, s_send_sem, s_recv_sem):
    n_chunks = out_ref.shape[0]
    rep = lax.axis_index("rep")
    shard = lax.axis_index("shard")
    y, c = shard // 2, shard % 2
    nbits = int(math.log2(n_rep))
    bits = [(rep // (1 << b)) % 2 for b in range(nbits)]

    def rep_peer(b):
        return (rep + (1 << b) * (1 - 2 * bits[b]), shard)

    core_peer = (rep, shard + 1 - 2 * c)
    y_peer = (rep, shard + 2 - 4 * y)
    halving = list(range(min(3, nbits)))
    extra = list(range(min(3, nbits), nbits))
    sizes = [BLK >> (k + 1) for k in range(len(halving))]

    def base(k):
        off = 0
        for j in range(k):
            off = off + bits[halving[j]] * sizes[j]
        return off

    loads = [
        pltpu.make_async_copy(src, dst.at[:, pl.ds(first, src.shape[1])], load_sem.at[j])
        for j, (src, dst, first) in enumerate([
            (normed_hbm, left, 0), (gh_hbm, right, 4 * D), (active_hbm, left, 2 * D), (up_hbm, right, 3 * D),
            (attended_hbm, left, D), (gm_hbm, right, 0)])]
    for load in loads:
        load.start()

    barrier = pltpu.get_barrier_semaphore()
    peers = [core_peer, y_peer] + [rep_peer(b) for b in range(nbits)]
    for p in peers:
        pl.semaphore_signal(barrier, inc=1, device_id=p, device_id_type=MESH)
    pl.semaphore_wait(barrier, len(peers))

    def copy(src, dst, stage, slot, peer):
        return pltpu.make_async_remote_copy(
            src_ref=src, dst_ref=dst, send_sem=send_sem.at[stage, slot],
            recv_sem=recv_sem.at[stage, slot], device_id=peer, device_id_type=MESH)

    def core_copy(t):
        s = t % SLOTS
        return copy(c_send.at[s], c_recv.at[s], 0, s, core_peer)

    def y_copy(t):
        s = t % SLOTS
        return copy(y_send.at[s], y_recv.at[s], 1, s, y_peer)

    def half_copy(k, t):
        s = t % SLOTS
        rows = sizes[k]
        start = pl.multiple_of(base(k) + (1 - bits[halving[k]]) * rows, 16)
        return copy(work.at[s, pl.ds(start, rows)], recvs[k].at[s], 2 + k, s, rep_peer(halving[k]))

    last = len(halving)

    def own():
        return pl.multiple_of(base(last), 16)

    tail = BLK >> last

    def extra_copy(j, t):
        s = t % SLOTS
        return copy(work.at[s, pl.ds(own(), tail)], recvs[last + j].at[s], 2 + last + j, s, rep_peer(extra[j]))

    def gather_copy(k, t):
        s = t % SLOTS
        rows = sizes[k]
        start = pl.multiple_of(base(k) + bits[halving[k]] * rows, 16)
        ref = out_ref.at[t, pl.ds(start, rows)]
        return copy(ref, ref, 2 + last + len(extra) + k, s, rep_peer(halving[k]))

    def compute(t):
        s = t % SLOTS
        for at, ready in ((0, loads[:2]), (16, loads[2:4]), (32, loads[4:])):
            @pl.when(t == at)
            def _(ready=ready):
                for load in ready:
                    load.wait()
        first, stride, column, new = chunk_plan(t)

        @pl.when(new)
        def _():
            for o in range(4):
                at = pl.multiple_of(first + o * stride, BLK)
                turned[o % 2, (o // 2) * BLK:(o // 2 + 1) * BLK, :] = left[:, pl.ds(at, BLK)].T
        operand = right[:, pl.ds(pl.multiple_of(column, COL), COL)]
        for side, dst in ((1 - c, c_send), (c, c_keep)):
            part = jnp.dot(turned[side], operand, preferred_element_type=jnp.float32)
            dst[s] = part.astype(jnp.bfloat16).reshape(2, BLK, COL)
        core_copy(t).start()

    def after_core(t):
        s = t % SLOTS
        core_copy(t).wait()
        y_send[s] = c_keep[s, 1 - y] + c_recv[s, 1 - y]
        y_copy(t).start()
        y_keep[s] = c_keep[s, y] + c_recv[s, y]

    def after_y(t):
        s = t % SLOTS
        y_copy(t).wait()
        work[s] = y_keep[s] + y_recv[s]
        half_copy(0, t).start()

    def after_half(k, t):
        s = t % SLOTS
        half_copy(k, t).wait()
        rows = sizes[k]
        start = pl.multiple_of(base(k + 1), 16)
        total = work[s, pl.ds(start, rows)] + recvs[k][s]
        if k + 1 < last:
            work[s, pl.ds(start, rows)] = total
            half_copy(k + 1, t).start()
        elif extra:
            work[s, pl.ds(start, rows)] = total
            extra_copy(0, t).start()
        else:
            out_ref[t, pl.ds(start, rows)] = total
            gather_copy(last - 1, t).start()

    def after_extra(j, t):
        s = t % SLOTS
        extra_copy(j, t).wait()
        total = work[s, pl.ds(own(), tail)] + recvs[last + j][s]
        if j + 1 < len(extra):
            work[s, pl.ds(own(), tail)] = total
            extra_copy(j + 1, t).start()
        else:
            out_ref[t, pl.ds(own(), tail)] = total
            gather_copy(last - 1, t).start()

    def after_gather(k, t):
        gather_copy(k, t).wait()
        if k > 0:
            gather_copy(k - 1, t).start()

    stages = [(0, compute), (LAGS[0], after_core), (LAGS[0]+LAGS[1], after_y)]
    lag = LAGS[0]+LAGS[1]
    for k in range(last):
        lag += LAGS[2+k]
        stages.append((lag, functools.partial(after_half, k)))
    for j in range(len(extra)):
        lag += 1
        stages.append((lag, functools.partial(after_extra, j)))
    for k in reversed(range(last)):
        lag += LAGS[5+last-1-k]
        stages.append((lag, functools.partial(after_gather, k)))

    s_peers = peers

    def small_copy(j):
        return pltpu.make_async_remote_copy(
            src_ref=s_buf.at[j], dst_ref=s_recv.at[j], send_sem=s_send_sem.at[j],
            recv_sem=s_recv_sem.at[j], device_id=s_peers[j], device_id_type=MESH)

    def small_step(j):
        if j == 0:
            s_buf[0] = small_ref[...]
        else:
            small_copy(j - 1).wait()
            total = s_buf[j - 1] + s_recv[j - 1]
            if j < len(s_peers):
                s_buf[j] = total
            else:
                small_out[...] = total
        if j < len(s_peers):
            small_copy(j).start()

    def step(i, carry):
        for delay, stage in reversed(stages):
            @pl.when((i >= delay) & (i < n_chunks + delay))
            def _(stage=stage, delay=delay):
                stage(i - delay)
        for j in range(len(s_peers) + 1):
            @pl.when(i == 4 + j)
            def _(j=j):
                small_step(j)
        return carry

    lax.fori_loop(0, n_chunks + lag, step, 0)


def grad_reduce(operands, small, n_rep, n_chunks):
    nbits = int(math.log2(n_rep))
    last = min(3, nbits)
    n_extra = nbits - last
    n_stage = 2 + last + n_extra + last
    bf = jnp.bfloat16
    recv_rows = [BLK >> (k + 1) for k in range(last)] + [BLK >> last] * n_extra
    chunk = (SLOTS, BLK, COL)
    pair = (SLOTS, 2, BLK, COL)
    n_small = 2 + nbits

    def kern(*refs):
        fixed, rest = refs[:20], refs[20:]
        recvs = rest[:len(recv_rows)]
        reduce_kernel(n_rep, *fixed, recvs, *rest[len(recv_rows):])

    tokens = operands[0].shape[0]
    hbm = pl.BlockSpec(memory_space=pl.ANY)
    vm = pl.BlockSpec(memory_space=pltpu.VMEM)
    return pl.pallas_call(
        kern,
        out_shape=(jax.ShapeDtypeStruct((n_chunks, BLK, COL), bf), jax.ShapeDtypeStruct(small.shape, jnp.float32)),
        in_specs=[hbm] * 6 + [vm],
        out_specs=(vm, vm),
        scratch_shapes=[
            pltpu.VMEM((tokens, 6 * D), bf), pltpu.VMEM((tokens, 8 * D), bf), pltpu.VMEM((2, 2 * BLK, tokens), bf),
            pltpu.SemaphoreType.DMA((6,)),
            pltpu.VMEM(pair, bf), pltpu.VMEM(pair, bf), pltpu.VMEM(pair, bf),
            pltpu.VMEM(chunk, bf), pltpu.VMEM(chunk, bf), pltpu.VMEM(chunk, bf), pltpu.VMEM(chunk, bf),
            *[pltpu.VMEM((SLOTS, rows, COL), bf) for rows in recv_rows],
            pltpu.VMEM((n_small,) + small.shape, jnp.float32), pltpu.VMEM((n_small,) + small.shape, jnp.float32),
            pltpu.SemaphoreType.DMA((n_stage, SLOTS)), pltpu.SemaphoreType.DMA((n_stage, SLOTS)),
            pltpu.SemaphoreType.DMA((n_small,)), pltpu.SemaphoreType.DMA((n_small,)),
        ],
        compiler_params=pltpu.CompilerParams(collective_id=1, has_side_effects=True, vmem_limit_bytes=60 * 2**20),
        name="grad_reduce",
    )(*operands, small)


def chunk_plan(t):
    cases = [
        ((t // 8) * BLK, D // 4, 4 * D + (t % 8) * COL, t % 8),
        (2 * D + ((t - 16) // 2) * BLK, D, 3 * D + (t % 2) * COL, t % 2),
        (((t - 32) // 6) * BLK, D // 4, ((t - 32) % 6) * COL, (t - 32) % 6),
        (D + ((t - 44) // 2) * BLK, D // 4, 3 * D + (t % 2) * COL, t % 2),
    ]
    first, stride, column, within = (
        jnp.where(t < 16, cases[0][i], jnp.where(t < 32, cases[1][i], jnp.where(t < 44, cases[2][i], cases[3][i])))
        for i in range(4))
    return first, stride, column, within == 0


def assemble(blocks, first, rows, cols, width, scale):
    def kern(in_ref, out_ref):
        for j in range(width):
            out_ref[:, j * COL:(j + 1) * COL] = in_ref[j].astype(jnp.float32) * scale

    across = cols // COL // width
    return pl.pallas_call(
        kern,
        grid=(rows // BLK, across),
        out_shape=jax.ShapeDtypeStruct((rows, cols), jnp.float32),
        in_specs=[pl.BlockSpec((width, BLK, COL), lambda i, j: (first // width + i * across + j, 0, 0))],
        out_specs=pl.BlockSpec((BLK, width * COL), lambda i, j: (i, j)),
        name="assemble",
    )(blocks)


def body(
    tokens,
    positions,
    lengths,
    owner,
    qkv_weight,
    out_weight,
    in_weight,
    in_bias,
    fc_weight,
    fc_bias,
    norm_gain,
    norm_bias,
    cotangent,
):
    rep_count = lax.axis_size("rep")
    shard_count = lax.axis_size("shard")
    device = lax.axis_index(("rep", "shard"))
    shard = lax.axis_index("shard")
    grad_scale = 1.0 / math.sqrt(TOK_DEV * rep_count * shard_count)
    segment, in_use = layout(lengths, owner, device)
    tables = rotary_tables(positions)
    upstream = cotangent * in_use[:, None].astype(jnp.bfloat16)
    small = jnp.concatenate([in_bias, fc_bias, norm_gain, norm_bias, jnp.zeros((256,), jnp.bfloat16)])
    small = small.astype(jnp.float32).reshape(16, 128)
    normed, active, grad_hidden, rows, base, grad_ff, grad_attended, grad_in_bias, norms, qkv_full, out_full = front(
        tokens, upstream, tables, small, in_weight, fc_weight, qkv_weight, out_weight, shard_count)
    attended, grad_merged = attention(rows, grad_attended, segment, tables)
    layer_out = (base + jnp.dot(attended, out_full, preferred_element_type=jnp.float32)).astype(jnp.bfloat16)
    grad_normed = grad_ff + jnp.einsum("te,de->td", grad_merged, qkv_full, preferred_element_type=jnp.float32)
    inputs = tokens.astype(jnp.float32)
    upstream_wide = upstream.astype(jnp.float32)
    _, norm_back = jax.vjp(layer_norm, inputs, norms[0], norms[1])
    grad_inputs, grad_gain, grad_shift = norm_back(grad_normed)
    input_grad = (grad_inputs + upstream_wide).astype(jnp.bfloat16)
    grad_fc_bias = jnp.sum(upstream_wide, axis=0)
    small_grads = jnp.concatenate([grad_in_bias[0], grad_fc_bias, grad_gain, grad_shift]).reshape(-1, 128)
    blocks, small_sum = grad_reduce(
        (normed, attended, active, grad_merged, upstream, grad_hidden), small_grads, rep_count, 48)
    small_sum = small_sum.reshape(-1) * grad_scale

    def own_part(first, size):
        return lax.dynamic_slice_in_dim(small_sum, first + shard * (size // 4), size // 4)

    return (
        layer_out,
        input_grad,
        assemble(blocks, 32, 256, 3 * D, 2, grad_scale),
        assemble(blocks, 44, 256, D, 2, grad_scale),
        assemble(blocks, 0, 256, 4 * D, 8, grad_scale),
        own_part(0, 4096),
        assemble(blocks, 16, 1024, D, 2, grad_scale),
        own_part(4096, D),
        own_part(4096 + D, D),
        own_part(4096 + 2 * D, D),
    )


def solution(mesh):
    in_specs = (
        P(("rep", "shard"), None),
        P(("rep", "shard")),
        P(),
        P(),
        P("shard", None),
        P("shard", None),
        P("shard", None),
        P("shard"),
        P("shard", None),
        P("shard"),
        P("shard"),
        P("shard"),
        P(("rep", "shard"), None),
    )
    out_specs = (
        P(("rep", "shard"), None),
        P(("rep", "shard"), None),
        P("shard", None),
        P("shard", None),
        P("shard", None),
        P("shard"),
        P("shard", None),
        P("shard"),
        P("shard"),
        P("shard"),
    )
    return jax.shard_map(body, mesh=mesh, in_specs=in_specs, out_specs=out_specs, check_vma=False)
```

profile of v0, /device:TPU:0, one launch (start us, length us, event | category | flops | bytes accessed | tf_op | source)
XLA Modules:
  0.0 336.6 jit_solution(9565385029945213081)
XLA Ops:
  0.6 0.0 copy-start.9
  0.7 0.7 fusion.15
  1.4 1.3 fusion.17
  2.7 0.6 fusion.13
  3.4 0.7 convert_element_type.44
  4.1 1.4 convert_reduce_fusion.1
  5.5 0.7 constant_dynamic-update-slice_fusion
  6.2 0.8 dynamic-update-slice.1
  7.0 0.8 dynamic-update-slice.2
  7.9 0.8 dynamic-update-slice.3
  8.7 0.2 dynamic-update-slice.4
  8.9 0.6 bitcast_convert_fusion.small_ref
  9.5 0.1 copy.26
  9.6 0.1 reduce-window.8
  9.7 0.1 reduce
  9.8 0.1 convert_reduce_fusion.2
  9.9 0.7 compare_select_fusion.seg_row
  10.6 0.1 copy.27
  10.7 0.7 add_select_fusion.seg_col
  11.4 1.9 fusion.9
  13.3 0.0 copy-done.9
  13.3 1.3 convert_reduce_fusion
  14.6 95.7 %front.1 = (bf16[512,1024]{1,0:T(8,128)(2,1)}, bf16[512,4096]{1,0:T(8,128)(2,1)}, bf16[512,4096]{1,0:T(8,128)(2,1)}, bf16[512,3072]{1,0:T(8,128)(2,1)}, f32[512,...) custom-call(bf16[512,1024]{1,0:T(8,128)(2,1)} %tok_ref.1, ...), custom_call_target="tpu_custom_call" | custom-call | tf_op jit(solution)/shard_map/front/pallas_call | solution.py:289
  110.3 0.8 slice.3
  111.1 0.0 copy-done
  111.1 0.0 copy-done.1
  111.1 0.0 copy-done.2
  111.1 0.0 copy-start.4
  111.1 1.2 copy-done.4
  112.3 23.8 %attention.1 = (bf16[512,1024]{1,0:T(8,128)(2,1)S(1)}, bf16[512,3072]{1,0:T(8,128)(2,1)}) custom-call(bf16[512,3072]{1,0:T(8,128)(2,1)} %get-tuple-element.26.q_ref.k_ref.v_ref, bf16[512,3072]{1,0:T(8,128)(2,1)} %get-tuple-element.26.q_ref.k_ref.v_ref, bf16[512,3072]{1,0:T(8,128)(2,1)} %get-tuple-element.26.q_ref.k_ref.v_ref, ...), custom_call_target="tpu_custom_call" | custom-call | tf_op jit(solution)/shard_map/attention/pallas_call | solution.py:381
  136.2 6.7 %fusion.4 = (f32[512]{0:T(512)S(1)}, f32[512]{0:T(512)S(1)}, f32[512,1024]{1,0:T(8,128)S(1)}) fusion(bf16[512,1024]{1,0:T(8,128)(2,1)S(1)} %copy-done.5, f32[512]{0:T(512)S(1)} %broadcast_multiply_fusion.1, f32[1024]{0:T(1024)S(1)} %bitcast.17, f32[512,1024]{1,0:T(8,128)} %get-tuple-element.30, bf16[512,3072]{1,0:T(8,128)(2,1)} %get-tuple-element.31.refs_3_, ...), kind=kOutput, calls=%fused_computation.9 | convolution fusion | flops 3225418752 | bytes 14690304 | tf_op jit(solution)/shard_map/te,de->td/dot_general | solution.py:681
  142.9 0.0 copy-done.3
  142.9 0.0 copy-done.12
  142.9 0.0 copy-done.13
  142.9 2.2 add_convert_fusion
  145.1 0.0 copy-done.8
  145.2 1.0 fusion.7
  146.2 0.6 maximum_bitcast_fusion.refs_6_
  146.8 168.3 %grad_reduce.1 = (bf16[48,128,512]{2,1,0:T(8,128)(2,1)}, f32[56,128]{1,0:T(8,128)}) custom-call(bf16[512,1024]{1,0:T(8,128)(2,1)} %get-tuple-element.34.refs_0_, bf16[512,1024]{1,0:T(8,128)(2,1)} %copy-done.3, bf16[512,4096]{1,0:T(8,128)(2,1)} %get-tuple-element.35.refs_2_, bf16[512,3072]{1,0:T(8,128)(2,1)} %get-tuple-element.31.refs_3_, ...), custom_call_target="tpu_custom_call" | custom-call | tf_op jit(solution)/shard_map/grad_reduce/pallas_call | solution.py:603
  315.1 0.8 multiply_bitcast_fusion
  315.9 0.6 fusion.20
  316.5 0.6 dynamic_slice.12
  317.1 0.0 copy-done.7
  317.1 3.3 fusion.8
  320.5 2.0 assemble.5
  322.4 4.8 %assemble.4 = f32[256,3072]{1,0:T(8,128)} custom-call(bf16[48,128,512]{2,1,0:T(8,128)(2,1)} %get-tuple-element.38.in_ref), custom_call_target="tpu_custom_call" | custom-call | tf_op jit(solution)/shard_map/assemble/pallas_call | solution.py:642
  327.2 6.0 %assemble.7 = f32[1024,1024]{1,0:T(8,128)} custom-call(bf16[48,128,512]{2,1,0:T(8,128)(2,1)} %get-tuple-element.38.in_ref), custom_call_target="tpu_custom_call" | custom-call | tf_op jit(solution)/shard_map/assemble/pallas_call | solution.py:642
  333.2 3.4 %assemble.6 = f32[256,4096]{1,0:T(8,128)} custom-call(bf16[48,128,512]{2,1,0:T(8,128)(2,1)} %get-tuple-element.38.in_ref), custom_call_target="tpu_custom_call" | custom-call | tf_op jit(solution)/shard_map/assemble/pallas_call | solution.py:642
  (22 shorter events, 0.1 us)
Async XLA Ops:
  0.6 12.7 %copy-start.9 = (bf16[512,1024]{1,0:T(8,128)(2,1)S(1)}, bf16[512,1024]{1,0:T(8,128)(2,1)}, u32[]{:S(2)}) copy-start(bf16[512,1024]{1,0:T(8,128)(2,1)} %param.25) | copy-start | bytes 3145732
  14.6 96.5 %copy-start = (f32[512,128]{1,0:T(8,128)S(1)}, f32[512,128]{1,0:T(8,128)}, u32[]{:S(2)}) copy-start(f32[512,128]{1,0:T(8,128)} %get-tuple-element.50.sb_ref) | copy-start | bytes 786436
  14.6 96.5 %copy-start.1 = (f32[512,128]{1,0:T(8,128)S(1)}, f32[512,128]{1,0:T(8,128)}, u32[]{:S(2)}) copy-start(f32[512,128]{1,0:T(8,128)} %get-tuple-element.51.sa_ref) | copy-start | bytes 786436
  14.6 96.5 %copy-start.2 = (f32[512,128]{1,0:T(8,128)S(1)}, f32[512,128]{1,0:T(8,128)}, u32[]{:S(2)}) copy-start(f32[512,128]{1,0:T(8,128)} %get-tuple-element.52.cos_ref) | copy-start | bytes 786436
  111.1 1.2 copy-start.4
  112.3 23.8 %copy-start.5 = (bf16[512,1024]{1,0:T(8,128)(2,1)S(1)}, bf16[512,1024]{1,0:T(8,128)(2,1)}, u32[]{:S(2)}) copy-start(bf16[512,1024]{1,0:T(8,128)(2,1)} %tok_ref.1) | copy-start | bytes 3145732
  112.3 23.8 %copy-start.11 = (bf16[1024,3072]{1,0:T(8,128)(2,1)S(1)}, bf16[1024,3072]{1,0:T(8,128)(2,1)}, u32[]{:S(2)}) copy-start(bf16[1024,3072]{1,0:T(8,128)(2,1)} %get-tuple-element.32) | copy-start | bytes 18874372
  136.1 6.7 %copy-start.3 = (bf16[512,1024]{1,0:T(8,128)(2,1)}, bf16[512,1024]{1,0:T(8,128)(2,1)S(1)}, u32[]{:S(2)}) copy-start(bf16[512,1024]{1,0:T(8,128)(2,1)S(1)} %get-tuple-element.28.refs_1_) | copy-start | bytes 3145732
  136.2 6.7 %copy-start.12 = (f32[512,1024]{1,0:T(8,128)S(1)}, f32[512,1024]{1,0:T(8,128)}, u32[]{:S(2)}) copy-start(f32[512,1024]{1,0:T(8,128)} %get-tuple-element.25) | copy-start | bytes 6291460
  136.2 6.7 %copy-start.13 = (bf16[1024,1024]{1,0:T(8,128)(2,1)S(1)}, bf16[1024,1024]{1,0:T(8,128)(2,1)}, u32[]{:S(2)}) copy-start(bf16[1024,1024]{1,0:T(8,128)(2,1)} %get-tuple-element.29) | copy-start | bytes 6291460
  142.9 2.3 copy-start.8
  145.1 1.1 copy-start.10
  146.8 170.3 %copy-start.6 = (bf16[512,1024]{1,0:T(8,128)(2,1)S(1)}, bf16[512,1024]{1,0:T(8,128)(2,1)}, u32[]{:S(2)}) copy-start(bf16[512,1024]{1,0:T(8,128)(2,1)} %tok_ref.1) | copy-start | bytes 3145732
  146.8 170.3 %copy-start.7 = (bf16[512,1024]{1,0:T(8,128)(2,1)S(1)}, bf16[512,1024]{1,0:T(8,128)(2,1)}, u32[]{:S(2)}) copy-start(bf16[512,1024]{1,0:T(8,128)(2,1)} %get-tuple-element.46.up_ref.refs_4_) | copy-start | bytes 3145732
where the time goes:
time: 337 us
  Pallas kernels  304 us (90%)
  other arithmetic  16 us (5%)
  matrix products  8.92 us (3%)
  local copies, waits for them, and re-layouts  6.89 us (2%)
    pallas_call x1, Pallas kernels, grad_reduce(): pl.pallas_call(kern, out_shape=(jax.ShapeDtypeStruct((n_chunks, BLK, COL)...  168 us
    pallas_call x1, Pallas kernels, front(): pl.pallas_call(front_kernel, out_shape=[jax.ShapeDtypeStruct(s, d) for s,...  95.7 us
    pallas_call x1, Pallas kernels, attention(): pl.pallas_call(attention_kernel, grid=(pairs,), out_shape=[jax.ShapeDtype...  23.8 us
    pallas_call x4, Pallas kernels, assemble(): pl.pallas_call(kern, grid=(rows // BLK, across), out_shape=jax.ShapeDtype...  16.1 us

commit v1 on v0

--- a/solution.py
+++ b/solution.py
@@ -40,12 +40,6 @@
     return (jnp.where(in_use, segment, TOK_DEV + slot_index), in_use)
 
 
-def layer_norm(inputs, scale_gain, norm_shift):
-    center = inputs - jnp.mean(inputs, axis=-1, keepdims=True)
-    spread = jnp.mean(center * center, axis=-1, keepdims=True)
-    return center * lax.rsqrt(spread + EPS) * scale_gain + norm_shift
-
-
 def rotary_tables(positions):
     lane = jnp.arange(128, dtype=jnp.int32) % HEAD_DIM
     rotated = lane < ROT_DIM
@@ -60,11 +54,11 @@
 FBLK = 256
 
 
-def front_kernel(tok_ref, up_ref, cos_ref, sa_ref, sb_ref, small_ref, in_own, fc_own, qkv_own, out_own,
-                 normed_ref, active_ref, gh_ref, rows_ref, base_ref, gn_ref, ga_ref, gib_ref, norm_ref,
-                 qkv_full, out_full,
-                 in_full, fc_full, small_full, bias_ref,
-                 send_sem, recv_sem, core_send, core_recv, own_send, own_recv, local_sem, s_send, s_recv):
+def front_kernel(tok_ref, up_ref, small_ref, in_own, fc_own, qkv_own, out_own,
+                 normed_out, active_out, gh_out, base_out, gn_out, gib_ref, norm_ref, qkv_full, out_full,
+                 in_full, fc_full, qkv_stage, out_stage, normed_ref, active_ref, gh_ref, base_ref, gn_ref,
+                 small_full, bias_ref,
+                 send_sem, recv_sem, core_send, core_recv, own_send, own_recv, local_sem, store_sem, s_send, s_recv):
     rep = lax.axis_index("rep")
     shard = lax.axis_index("shard")
     y, c = shard // 2, shard % 2
@@ -133,8 +127,18 @@
     def own_copy(a):
         return remote(owns[a], own_rows(a), (own_send, own_recv), (a,), core_peer)
 
+    stages = (None, None, qkv_stage, out_stage)
+
     def local_copy(a):
-        return pltpu.make_async_copy(owns[a], own_rows(a), local_sem.at[a])
+        return pltpu.make_async_copy(owns[a], own_rows(a) if stages[a] is None else stages[a], local_sem.at[a])
+
+    def stage_copy(a):
+        return pltpu.make_async_copy(stages[a], own_rows(a), local_sem.at[a + 2])
+
+    results = [(normed_ref, normed_out), (active_ref, active_out), (gh_ref, gh_out), (base_ref, base_out), (gn_ref, gn_out)]
+
+    def store(j):
+        return pltpu.make_async_copy(results[j][0], results[j][1], store_sem.at[j])
 
     def small_copy(j):
         return remote(small_ref, small_full.at[shard], (s_send, s_recv), (j,), group[j])
@@ -200,25 +204,6 @@
         gn_ref[:, at] = lax.dot_general(gh_ref[...], in_full[at, :], (((1,), (1,)), ((), ())), preferred_element_type=jnp.float32)
         return carry
 
-    def turn_block(j, carry):
-        at = span(j)
-        rows = jnp.dot(normed_ref[...], qkv_full[:, at], preferred_element_type=jnp.float32)
-        for g in range(FBLK // 128):
-            part = rows[:, g * 128:(g + 1) * 128]
-            turned = part * cos_ref[...] + pltpu.roll(part, 127, 1) * sa_ref[...] + pltpu.roll(part, 1, 1) * sb_ref[...]
-            rows_ref[:, pl.ds(pl.multiple_of(j * FBLK + g * 128, 128), 128)] = turned.astype(jnp.bfloat16)
-        return carry
-
-    def value_block(j, carry):
-        at = span(j)
-        rows_ref[:, at] = jnp.dot(normed_ref[...], qkv_full[:, at], preferred_element_type=jnp.float32).astype(jnp.bfloat16)
-        return carry
-
-    def out_block(j, carry):
-        at = span(j)
-        ga_ref[:, at] = lax.dot_general(up_ref[...], out_full[at, :], (((1,), (1,)), ((), ())), preferred_element_type=jnp.float32).astype(jnp.bfloat16)
-        return carry
-
     def loop(block, lo, hi):
         lax.fori_loop(lo, hi, block, 0)
 
@@ -234,15 +219,24 @@
     def plan(step, *todo):
         work.setdefault(step, []).extend(todo)
 
-    plan(ends[0], functools.partial(ready, 0))
+    def unstage():
+        for a in (2, 3):
+            local_copy(a).wait()
+            stage_copy(a).start()
+
+    bind = functools.partial
+    plan(2, unstage, lambda: store(0).start())
+    plan(ends[0], bind(ready, 0))
     for j in range(4):
-        plan(ends[0] + j, functools.partial(loop, hidden_block, j * nf // 4, (j + 1) * nf // 4))
-    plan(ends[1], functools.partial(ready, 1))
-    for j in range(4):
-        plan(ends[1] + j, functools.partial(loop, back_block, j * nf // 4, (j + 1) * nf // 4))
-    plan(ends[2], functools.partial(ready, 2), functools.partial(loop, mlp_block, 0, D // FBLK),
-         functools.partial(loop, turn_block, 0, 2 * D // FBLK), functools.partial(loop, value_block, 2 * D // FBLK, 3 * D // FBLK))
-    plan(ends[3], functools.partial(ready, 3), functools.partial(loop, out_block, 0, D // FBLK))
+        plan(ends[0] + j, bind(loop, hidden_block, j * nf // 4, (j + 1) * nf // 4))
+    plan(ends[0] + 3, lambda: store(1).start())
+    plan(ends[1], bind(ready, 1))
+    for j in range(3):
+        plan(ends[1] + j, bind(loop, back_block, j * nf // 4, (j + 1) * nf // 4))
+    plan(ends[1] + 3, bind(loop, back_block, 3 * nf // 4, nf), lambda: store(2).start())
+    nd = D // FBLK
+    plan(ends[1] + 4, bind(loop, mlp_block, 0, nd // 2))
+    plan(ends[1] + 5, bind(loop, mlp_block, nd // 2, nd), lambda: store(3).start(), lambda: store(4).start())
 
     for i in range(n + lag[3]):
         if i < n:
@@ -269,9 +263,14 @@
         core_copy(i).wait_send()
     for a in range(4):
         own_copy(a).wait_send()
-
-
-def front(tokens, upstream, tables, small, in_own, fc_own, qkv_own, out_own, shards):
+    for a in (2, 3):
+        own_copy(a).wait_recv()
+        stage_copy(a).wait()
+    for j in range(len(results)):
+        store(j).wait()
+
+
+def front(tokens, upstream, small, in_own, fc_own, qkv_own, out_own, shards):
     bf, f32 = jnp.bfloat16, jnp.float32
     rows = tokens.shape[0]
     ff = in_own.shape[1]
@@ -281,45 +280,31 @@
 
     def full(own):
         return (own.shape[0] * shards, own.shape[1])
-    out_shape = [
-        ((rows, D), bf), ((rows, ff), bf), ((rows, ff), bf), ((rows, 3 * D), bf), ((rows, D), f32), ((rows, D), f32),
-        ((rows, D), bf), ((1, ff), f32), ((8, D), f32), (full(qkv_own), bf), (full(out_own), bf),
-    ]
+    held = [((rows, D), bf), ((rows, ff), bf), ((rows, ff), bf), ((rows, D), f32), ((rows, D), f32)]
+    out_shape = held + [((1, ff), f32), ((8, D), f32), (full(qkv_own), bf), (full(out_own), bf)]
     dma = pltpu.SemaphoreType.DMA
     return pl.pallas_call(
         front_kernel,
         out_shape=[jax.ShapeDtypeStruct(s, d) for s, d in out_shape],
-        in_specs=[vm] * 6 + [hbm] * 4,
-        out_specs=[vm] * len(out_shape),
+        in_specs=[vm] * 3 + [hbm] * 4,
+        out_specs=[hbm] * 5 + [vm] * 2 + [hbm] * 2,
         scratch_shapes=[
             pltpu.VMEM(full(in_own), bf), pltpu.VMEM(full(fc_own), bf),
+            pltpu.VMEM(qkv_own.shape, bf), pltpu.VMEM(out_own.shape, bf),
+            *[pltpu.VMEM(s, d) for s, d in held],
             pltpu.VMEM((shards,) + small.shape, f32), pltpu.VMEM((1, ff), f32),
-            dma((3, n, 2)), dma((3, n, 2)), dma((n,)), dma((n,)), dma((4,)), dma((4,)), dma((4,)), dma((3,)), dma((3,)),
+            dma((3, n, 2)), dma((3, n, 2)), dma((n,)), dma((n,)), dma((4,)), dma((4,)), dma((6,)), dma((5,)),
+            dma((3,)), dma((3,)),
         ],
         compiler_params=pltpu.CompilerParams(collective_id=2, has_side_effects=True, vmem_limit_bytes=62 * 2**20),
         name="front",
-    )(tokens, upstream, *tables, small, in_own, fc_own, qkv_own, out_own)
-
-
-def attention_kernel(q_ref, k_ref, v_ref, ga_ref, seg_col, seg_row, cos_ref, sa_ref, sb_ref, att_ref, gm_ref, bias_ref):
-    pair = pl.program_id(0)
-
-    @pl.when(pair == 0)
-    def _():
-        row = lax.broadcasted_iota(jnp.int32, (TOK_DEV, TOK_DEV), 0)
-        col = lax.broadcasted_iota(jnp.int32, (TOK_DEV, TOK_DEV), 1)
-        allowed = (seg_col[...] == seg_row[...]) & (col <= row)
-        bias_ref[...] = jnp.where(allowed, 0.0, NEG)
-
-    attend_pair(pair, q_ref[...], k_ref[...], v_ref[...], ga_ref[...], bias_ref, cos_ref, sa_ref, sb_ref,
-                lambda value: att_ref.__setitem__(Ellipsis, value),
-                lambda part, value: gm_ref.__setitem__((slice(None), pl.ds(pl.multiple_of(part * D + pair * 128, 128), 128)), value))
+    )(tokens, upstream, small, in_own, fc_own, qkv_own, out_own)
 
 
 QBLK = 256
 
 
-def attend_pair(pair, q, k, v, ga, bias_ref, cos_ref, sa_ref, sb_ref, put_att, put_grad):
+def attend_pair(q, k, v, ga, bias_ref, cos_ref, sa_ref, sb_ref, put_att, put_grad):
     f32, bf = jnp.float32, jnp.bfloat16
     nt = (((1,), (1,)), ((), ()))
     tn = (((0,), (0,)), ((), ()))
@@ -373,29 +358,11 @@
     put_grad(2, jnp.concatenate([grad_v[b] for b in range(n_blocks)], 0).astype(bf))
 
 
-def attention(rows, ga, segment, tables):
-    bf = jnp.bfloat16
-    t = rows.shape[0]
-    pairs = HEADS // 2
-    whole = pl.BlockSpec(memory_space=pltpu.VMEM)
-    return pl.pallas_call(
-        attention_kernel,
-        grid=(pairs,),
-        out_shape=[jax.ShapeDtypeStruct((t, D), bf), jax.ShapeDtypeStruct((t, 3 * D), bf)],
-        in_specs=[
-            pl.BlockSpec((t, 128), lambda p: (0, p)), pl.BlockSpec((t, 128), lambda p: (0, pairs + p)),
-            pl.BlockSpec((t, 128), lambda p: (0, 2 * pairs + p)), pl.BlockSpec((t, 128), lambda p: (0, p)),
-            whole, whole, whole, whole, whole,
-        ],
-        out_specs=[pl.BlockSpec((t, 128), lambda p: (0, p)), pl.BlockSpec((t, 3 * D), lambda p: (0, 0))],
-        scratch_shapes=[pltpu.VMEM((t, t), jnp.float32)],
-        compiler_params=pltpu.CompilerParams(vmem_limit_bytes=48 * 2**20),
-        name="attention",
-    )(rows, rows, rows, ga, segment[:, None], segment[None, :], *tables)
-
-
-def reduce_kernel(n_rep, normed_hbm, attended_hbm, active_hbm, gm_hbm, up_hbm, gh_hbm, small_ref, out_ref, small_out,
-                  left, right, turned, load_sem, c_send, c_keep, c_recv, y_send, y_keep, y_recv, work, recvs, s_buf, s_recv,
+def reduce_kernel(n_rep, normed_hbm, gh_hbm, qkv_hbm, up_hbm, out_hbm, active_hbm, gn_hbm, base_hbm, tok_hbm,
+                  bias_ref, cos_ref, sa_ref, sb_ref, gib_ref, norm_ref,
+                  out_ref, small_out, layer_ref, grad_ref,
+                  left, right, turned, qkv_full, out_full, gn_ref, base_ref, tok_ref, load_sem,
+                  c_send, c_keep, c_recv, y_send, y_keep, y_recv, work, recvs, s_buf, s_recv,
                   send_sem, recv_sem, s_send_sem, s_recv_sem):
     n_chunks = out_ref.shape[0]
     rep = lax.axis_index("rep")
@@ -420,10 +387,10 @@
         return off
 
     loads = [
-        pltpu.make_async_copy(src, dst.at[:, pl.ds(first, src.shape[1])], load_sem.at[j])
-        for j, (src, dst, first) in enumerate([
-            (normed_hbm, left, 0), (gh_hbm, right, 4 * D), (active_hbm, left, 2 * D), (up_hbm, right, 3 * D),
-            (attended_hbm, left, D), (gm_hbm, right, 0)])]
+        pltpu.make_async_copy(src, dst, load_sem.at[j]) for j, (src, dst) in enumerate([
+            (normed_hbm, left.at[:, 0:D]), (gh_hbm, right.at[:, 4 * D:8 * D]), (qkv_hbm, qkv_full),
+            (up_hbm, right.at[:, 3 * D:4 * D]), (out_hbm, out_full), (active_hbm, left.at[:, 2 * D:6 * D]),
+            (gn_hbm, gn_ref), (base_hbm, base_ref), (tok_hbm, tok_ref)])]
     for load in loads:
         load.start()
 
@@ -470,13 +437,92 @@
         ref = out_ref.at[t, pl.ds(start, rows)]
         return copy(ref, ref, 2 + last + len(extra) + k, s, rep_peer(halving[k]))
 
+    def first_use(t, at, *which):
+        @pl.when(t == at)
+        def _():
+            for j in which:
+                loads[j].wait()
+
+    f32, bf = jnp.float32, jnp.bfloat16
+    nt = (((1,), (1,)), ((), ()))
+
+    def block(start, j, size=256):
+        return pl.ds(pl.multiple_of(start + j * size, size), size)
+
+    def turn_rows(u):
+        first_use(u, 0, 2)
+        for b in range(2):
+            rows = jnp.dot(left[:, 0:D], qkv_full[:, block(0, 2 * u + b)], preferred_element_type=f32)
+            for g in range(2):
+                part = rows[:, g * 128:(g + 1) * 128]
+                part = part * cos_ref[...] + pltpu.roll(part, 127, 1) * sa_ref[...] + pltpu.roll(part, 1, 1) * sb_ref[...]
+                right[:, block(0, 4 * u + 2 * b + g, 128)] = part.astype(bf)
+
+    def value_rows(u):
+        for b in range(2):
+            at = block(2 * D, 2 * u + b)
+            right[:, at] = jnp.dot(left[:, 0:D], qkv_full[:, at], preferred_element_type=f32).astype(bf)
+
+    def grad_attended(u):
+        first_use(u, 0, 3, 4)
+        for b in range(2):
+            part = lax.dot_general(right[:, 3 * D:4 * D], out_full[block(0, 2 * u + b), :], nt, preferred_element_type=f32)
+            left[:, block(D, 2 * u + b)] = part.astype(bf)
+
+    def attend(u):
+        @pl.when(u % 2 == 0)
+        def _():
+            pair = u // 2
+            spans = [block(k * D, pair, 128) for k in range(3)]
+            span = block(D, pair, 128)
+
+            def put_att(value):
+                left[:, span] = value
+
+            def put_grad(part, value):
+                right[:, spans[part]] = value
+            attend_pair(right[:, spans[0]], right[:, spans[1]], right[:, spans[2]], left[:, span],
+                        bias_ref, cos_ref, sa_ref, sb_ref, put_att, put_grad)
+
+    def grad_normed(u):
+        first_use(u, 0, 6)
+        at = block(0, u)
+        gn_ref[:, at] = gn_ref[:, at] + lax.dot_general(right[:, 0:3 * D], qkv_full[at, :], nt, preferred_element_type=f32)
+
+    def project(u):
+        first_use(u, 0, 7)
+        for b in range(2):
+            at = block(0, 2 * u + b)
+            layer_ref[:, at] = (base_ref[:, at] + jnp.dot(left[:, D:2 * D], out_full[:, at], preferred_element_type=f32)).astype(bf)
+
+    def norm_back(u):
+        first_use(u, 0, 8)
+
+        @pl.when(u == 0)
+        def _():
+            s_buf[0] = jnp.zeros(s_buf.shape[1:], f32)
+            s_buf[0, :, 0:4 * D] = gib_ref[...]
+        at = block(0, u, 64)
+        x = tok_ref[at, :].astype(f32)
+        center = x - jnp.mean(x, axis=-1, keepdims=True)
+        scale = lax.rsqrt(jnp.mean(center * center, axis=-1, keepdims=True) + EPS)
+        unit = center * scale
+        grad = gn_ref[at, :]
+        upstream = right[at, 3 * D:4 * D].astype(f32)
+        wide = grad * norm_ref[0:1, :]
+        lean = wide - jnp.mean(wide, axis=-1, keepdims=True) - unit * jnp.mean(wide * unit, axis=-1, keepdims=True)
+        grad_ref[at, :] = (lean * scale + upstream).astype(bf)
+        for k, value in enumerate((upstream, grad * unit, grad)):
+            span = slice((4 + k) * D, (5 + k) * D)
+            s_buf[0, :, span] = s_buf[0, :, span] + jnp.sum(value, axis=0, keepdims=True)
+
+    tasks = [(0, 4, turn_rows), (4, 2, value_rows), (6, 2, grad_attended), (8, 16, attend), (25, 4, grad_normed),
+             (29, 2, project), (33, 8, norm_back)]
+
     def compute(t):
         s = t % SLOTS
-        for at, ready in ((0, loads[:2]), (16, loads[2:4]), (32, loads[4:])):
-            @pl.when(t == at)
-            def _(ready=ready):
-                for load in ready:
-                    load.wait()
+        first_use(t, 0, 0, 1)
+        first_use(t, 16, 5)
         first, stride, column, new = chunk_plan(t)
 
         @pl.when(new)
@@ -555,9 +601,7 @@
             recv_sem=s_recv_sem.at[j], device_id=s_peers[j], device_id_type=MESH)
 
     def small_step(j):
-        if j == 0:
-            s_buf[0] = small_ref[...]
-        else:
+        if j > 0:
             small_copy(j - 1).wait()
             total = s_buf[j - 1] + s_recv[j - 1]
             if j < len(s_peers):
@@ -572,8 +616,12 @@
             @pl.when((i >= delay) & (i < n_chunks + delay))
             def _(stage=stage, delay=delay):
                 stage(i - delay)
+        for start, count, task in tasks:
+            @pl.when((i >= start) & (i < start + count))
+            def _(start=start, task=task):
+                task(i - start)
         for j in range(len(s_peers) + 1):
-            @pl.when(i == 4 + j)
+            @pl.when(i == 42 + j)
             def _(j=j):
                 small_step(j)
         return carry
@@ -581,7 +629,7 @@
     lax.fori_loop(0, n_chunks + lag, step, 0)
 
 
-def grad_reduce(operands, small, n_rep, n_chunks):
+def grad_reduce(stream, fixed, n_rep, n_chunks):
     nbits = int(math.log2(n_rep))
     last = min(3, nbits)
     n_extra = nbits - last
@@ -593,31 +641,34 @@
     n_small = 2 + nbits
 
     def kern(*refs):
-        fixed, rest = refs[:20], refs[20:]
-        recvs = rest[:len(recv_rows)]
-        reduce_kernel(n_rep, *fixed, recvs, *rest[len(recv_rows):])
-
-    tokens = operands[0].shape[0]
+        first = refs[:n_fixed]
+        reduce_kernel(n_rep, *first, refs[n_fixed:n_fixed + len(recv_rows)], *refs[n_fixed + len(recv_rows):])
+
+    n_fixed = len(stream) + len(fixed) + 4 + 9 + 7
+    tokens = stream[0].shape[0]
+    small = (1, 7 * D)
     hbm = pl.BlockSpec(memory_space=pl.ANY)
     vm = pl.BlockSpec(memory_space=pltpu.VMEM)
     return pl.pallas_call(
         kern,
-        out_shape=(jax.ShapeDtypeStruct((n_chunks, BLK, COL), bf), jax.ShapeDtypeStruct(small.shape, jnp.float32)),
-        in_specs=[hbm] * 6 + [vm],
-        out_specs=(vm, vm),
+        out_shape=(jax.ShapeDtypeStruct((n_chunks, BLK, COL), bf), jax.ShapeDtypeStruct(small, jnp.float32),
+                   jax.ShapeDtypeStruct((tokens, D), bf), jax.ShapeDtypeStruct((tokens, D), bf)),
+        in_specs=[hbm] * len(stream) + [vm] * len(fixed),
+        out_specs=(vm,) * 4,
         scratch_shapes=[
             pltpu.VMEM((tokens, 6 * D), bf), pltpu.VMEM((tokens, 8 * D), bf), pltpu.VMEM((2, 2 * BLK, tokens), bf),
-            pltpu.SemaphoreType.DMA((6,)),
+            *[pltpu.VMEM(x.shape, x.dtype) for x in (stream[2], stream[4], stream[6], stream[7], stream[8])],
+            pltpu.SemaphoreType.DMA((9,)),
             pltpu.VMEM(pair, bf), pltpu.VMEM(pair, bf), pltpu.VMEM(pair, bf),
             pltpu.VMEM(chunk, bf), pltpu.VMEM(chunk, bf), pltpu.VMEM(chunk, bf), pltpu.VMEM(chunk, bf),
             *[pltpu.VMEM((SLOTS, rows, COL), bf) for rows in recv_rows],
-            pltpu.VMEM((n_small,) + small.shape, jnp.float32), pltpu.VMEM((n_small,) + small.shape, jnp.float32),
+            pltpu.VMEM((n_small,) + small, jnp.float32), pltpu.VMEM((n_small,) + small, jnp.float32),
             pltpu.SemaphoreType.DMA((n_stage, SLOTS)), pltpu.SemaphoreType.DMA((n_stage, SLOTS)),
             pltpu.SemaphoreType.DMA((n_small,)), pltpu.SemaphoreType.DMA((n_small,)),
         ],
-        compiler_params=pltpu.CompilerParams(collective_id=1, has_side_effects=True, vmem_limit_bytes=60 * 2**20),
+        compiler_params=pltpu.CompilerParams(collective_id=1, has_side_effects=True, vmem_limit_bytes=63 * 2**20),
         name="grad_reduce",
-    )(*operands, small)
+    )(*stream, *fixed)
 
 
 def chunk_plan(t):
@@ -633,18 +684,29 @@
     return first, stride, column, within == 0
 
 
-def assemble(blocks, first, rows, cols, width, scale):
-    def kern(in_ref, out_ref):
-        for j in range(width):
-            out_ref[:, j * COL:(j + 1) * COL] = in_ref[j].astype(jnp.float32) * scale
-
-    across = cols // COL // width
+def assemble(blocks, places, scale):
+    def kern(in_ref, *rest):
+        outs, (stage, sem) = rest[:-2], rest[-2:]
+        copies = []
+        for (first, rows, cols), out in zip(places, outs):
+            across = cols // COL
+            for i in range(rows // BLK):
+                for j in range(across):
+                    t = first + i * across + j
+                    stage[t] = in_ref[t].astype(jnp.float32) * scale
+                    copies.append(pltpu.make_async_copy(
+                        stage.at[t], out.at[i * BLK:(i + 1) * BLK, j * COL:(j + 1) * COL], sem.at[t]))
+                    copies[-1].start()
+        for copy in copies:
+            copy.wait()
+
     return pl.pallas_call(
         kern,
-        grid=(rows // BLK, across),
-        out_shape=jax.ShapeDtypeStruct((rows, cols), jnp.float32),
-        in_specs=[pl.BlockSpec((width, BLK, COL), lambda i, j: (first // width + i * across + j, 0, 0))],
-        out_specs=pl.BlockSpec((BLK, width * COL), lambda i, j: (i, j)),
+        out_shape=[jax.ShapeDtypeStruct((rows, cols), jnp.float32) for _, rows, cols in places],
+        in_specs=[pl.BlockSpec(memory_space=pltpu.VMEM)],
+        out_specs=[pl.BlockSpec(memory_space=pl.ANY)] * len(places),
+        scratch_shapes=[pltpu.VMEM(blocks.shape, jnp.float32), pltpu.SemaphoreType.DMA((blocks.shape[0],))],
+        compiler_params=pltpu.CompilerParams(vmem_limit_bytes=32 * 2**20),
         name="assemble",
     )(blocks)
 
@@ -671,36 +733,32 @@
     grad_scale = 1.0 / math.sqrt(TOK_DEV * rep_count * shard_count)
     segment, in_use = layout(lengths, owner, device)
     tables = rotary_tables(positions)
+    slot_index = jnp.arange(tokens.shape[0], dtype=jnp.int32)
+    allowed = (segment[:, None] == segment[None, :]) & (slot_index[None, :] <= slot_index[:, None])
+    bias = jnp.where(allowed, 0.0, NEG)
     upstream = cotangent * in_use[:, None].astype(jnp.bfloat16)
-    small = jnp.concatenate([in_bias, fc_bias, norm_gain, norm_bias, jnp.zeros((256,), jnp.bfloat16)])
-    small = small.astype(jnp.float32).reshape(16, 128)
-    normed, active, grad_hidden, rows, base, grad_ff, grad_attended, grad_in_bias, norms, qkv_full, out_full = front(
-        tokens, upstream, tables, small, in_weight, fc_weight, qkv_weight, out_weight, shard_count)
-    attended, grad_merged = attention(rows, grad_attended, segment, tables)
-    layer_out = (base + jnp.dot(attended, out_full, preferred_element_type=jnp.float32)).astype(jnp.bfloat16)
-    grad_normed = grad_ff + jnp.einsum("te,de->td", grad_merged, qkv_full, preferred_element_type=jnp.float32)
-    inputs = tokens.astype(jnp.float32)
-    upstream_wide = upstream.astype(jnp.float32)
-    _, norm_back = jax.vjp(layer_norm, inputs, norms[0], norms[1])
-    grad_inputs, grad_gain, grad_shift = norm_back(grad_normed)
-    input_grad = (grad_inputs + upstream_wide).astype(jnp.bfloat16)
-    grad_fc_bias = jnp.sum(upstream_wide, axis=0)
-    small_grads = jnp.concatenate([grad_in_bias[0], grad_fc_bias, grad_gain, grad_shift]).reshape(-1, 128)
-    blocks, small_sum = grad_reduce(
-        (normed, attended, active, grad_merged, upstream, grad_hidden), small_grads, rep_count, 48)
+    small = sum(jnp.pad(part.astype(jnp.float32), (first, 2048 - first - part.shape[0])) for first, part in (
+        (0, in_bias), (1024, fc_bias), (1280, norm_gain), (1536, norm_bias))).reshape(16, 128)
+    normed, active, grad_hidden, base, grad_ff, grad_in_bias, norms, qkv_full, out_full = front(
+        tokens, upstream, small, in_weight, fc_weight, qkv_weight, out_weight, shard_count)
+    blocks, small_sum, layer_out, input_grad = grad_reduce(
+        (normed, grad_hidden, qkv_full, upstream, out_full, active, grad_ff, base, tokens),
+        (bias, *tables, grad_in_bias, norms), rep_count, 48)
     small_sum = small_sum.reshape(-1) * grad_scale
 
     def own_part(first, size):
         return lax.dynamic_slice_in_dim(small_sum, first + shard * (size // 4), size // 4)
 
+    grad_in, grad_fc, grad_qkv, grad_out = assemble(
+        blocks, ((0, 256, 4 * D), (16, 1024, D), (32, 256, 3 * D), (44, 256, D)), grad_scale)
     return (
         layer_out,
         input_grad,
-        assemble(blocks, 32, 256, 3 * D, 2, grad_scale),
-        assemble(blocks, 44, 256, D, 2, grad_scale),
-        assemble(blocks, 0, 256, 4 * D, 8, grad_scale),
+        grad_qkv,
+        grad_out,
+        grad_in,
         own_part(0, 4096),
-        assemble(blocks, 16, 1024, D, 2, grad_scale),
+        grad_fc,
         own_part(4096, D),
         own_part(4096 + D, D),
         own_part(4096 + 2 * D, D),

time: 337 us -> 275 us (0.82)
  Pallas kernels: 304 us -> 258 us
  matrix products: 8.92 us -> 0 us
  other arithmetic: 16 us -> 9.65 us
    pallas_call x5 -> x1, Pallas kernels: 39.9 us -> 5.09 us  [assemble(): pl.pallas_call(kern, out_shape=[jax.ShapeDtypeStruct((rows, cols), jnp.fl...]
    pallas_call x1, Pallas kernels: 95.7 us -> 79.6 us  [front(): pl.pallas_call(front_kernel, out_shape=[jax.ShapeDtypeStruct(s, d) for s,...]
    dot_general x2 -> x0, matrix products: 8.92 us -> none  [the longest x1 6.69 us: body(): jnp.einsum('te,de->td', grad_merged, qkv_full, preferred_element_type=jnp...]
    pallas_call x1, Pallas kernels: 168 us -> 173 us  [grad_reduce(): pl.pallas_call(kern, out_shape=(jax.ShapeDtypeStruct((n_chunks, BLK, COL)...]
    convert_element_type x2 -> x0, other arithmetic: 3.94 us -> none  [the longest x1 3.34 us: body(): input_grad = (grad_inputs + upstream_wide).astype(jnp.bfloat16)]
    reduce_sum x3 -> x0, other arithmetic: 3.74 us -> none  [the longest x1 1.43 us: layer_norm(): center = inputs - jnp.mean(inputs, axis=-1, keepdims=True)]
where the time goes in v1:
time: 275 us
  Pallas kernels  258 us (94%)
  other arithmetic  9.65 us (4%)
  local copies, waits for them, and re-layouts  6.02 us (2%)
    pallas_call x1, Pallas kernels, grad_reduce(): pl.pallas_call(kern, out_shape=(jax.ShapeDtypeStruct((n_chunks, BLK, COL)...  173 us
    pallas_call x1, Pallas kernels, front(): pl.pallas_call(front_kernel, out_shape=[jax.ShapeDtypeStruct(s, d) for s,...  79.6 us

profile of v1, /device:TPU:0, one launch (start us, length us, event | category | flops | bytes accessed | tf_op | source)
XLA Modules:
  0.0 274.6 jit_solution(7613428204980444088)
XLA Ops:
  0.6 0.0 copy-start.5
  0.7 0.0 copy-start.8
  0.7 0.0 copy-start.7
  0.7 0.0 copy-start.6
  0.7 1.3 fusion.9
  2.0 0.1 copy.25
  2.1 0.1 reduce-window.8
  2.2 0.1 reduce
  2.3 0.7 fusion.7
  3.0 0.1 convert_reduce_fusion
  3.1 0.7 add_select_fusion
  3.7 1.2 fusion.1.refs_9_
  4.9 0.6 fusion.6
  5.6 2.3 broadcast_multiply_fusion.up_ref.refs_3_
  7.9 0.0 copy-done.5
  7.9 0.0 copy-done.8
  7.9 0.0 copy-done.7
  7.9 0.0 copy-done.6
  7.9 0.6 add_bitcast_fusion.small_ref
  8.5 0.0 copy-start.4
  8.5 79.6 %front.1 = (bf16[512,1024]{1,0:T(8,128)(2,1)}, bf16[512,4096]{1,0:T(8,128)(2,1)}, bf16[512,4096]{1,0:T(8,128)(2,1)}, f32[512,1024]{1,0:T(8,128)}, f32[512,1024]{...) custom-call(bf16[512,1024]{1,0:T(8,128)(2,1)} %refs_8_.1, ...), custom_call_target="tpu_custom_call" | custom-call | tf_op jit(solution)/shard_map/front/pallas_call | solution.py:286
  88.2 0.0 copy-done.4
  88.2 1.9 fusion.2
  90.1 173.4 %grad_reduce.1 = (bf16[48,128,512]{2,1,0:T(8,128)(2,1)}, f32[1,7168]{1,0:T(1,128)}, bf16[512,1024]{1,0:T(8,128)(2,1)}, bf16[512,1024]{1,0:T(8,128)(2,1)}) custom-call(bf16[512,1024]{1,0:T(8,128)(2,1)} %get-tuple-element.27.refs_0_, bf16[512,4096]{1,0:T(8,128)(2,1)} %get-tuple-element.28.refs_1_, bf16[1024,3072]{1,0:T(8,128)(2,1)} %get-tuple-element.29.refs_2_, ...), custom_call_target="tpu_custom_call" | custom-call | tf_op jit(solution)/shard_map/grad_reduce/pallas_call | solution.py:652
  263.5 0.0 copy-start
  263.5 2.8 %copy-done = bf16[48,128,512]{2,1,0:T(8,128)(2,1)S(1)} copy-done((bf16[48,128,512]{2,1,0:T(8,128)(2,1)S(1)}, bf16[48,128,512]{2,1,0:T(8,128)(2,1)}, u32[]{:S(2)}) %copy-start) | copy-done | bytes 6291480
  266.3 0.0 copy-start.3
  266.3 0.0 copy-start.2
  266.3 0.0 copy-start.1
  266.3 5.1 %assemble.1 = (f32[256,4096]{1,0:T(8,128)}, f32[1024,1024]{1,0:T(8,128)}, f32[256,3072]{1,0:T(8,128)}, f32[256,1024]{1,0:T(8,128)}) custom-call(bf16[48,128,512]{2,1,0:T(8,128)(2,1)S(1)} %copy-done), custom_call_target="tpu_custom_call" | custom-call | tf_op jit(solution)/shard_map/assemble/pallas_call | solution.py:703
  271.4 0.0 copy-done.3
  271.4 0.6 constant_dynamic-slice_fusion
  272.0 0.6 constant_dynamic-slice_fusion.3
  272.6 0.0 copy-done.2
  272.6 1.0 copy.28
  273.6 0.0 copy-done.1
  273.6 1.0 copy.29
  (4 shorter events, 0.1 us)
Async XLA Ops:
  0.6 7.3 %copy-start.5 = (bf16[1024]{0:T(1024)(128)(2,1)S(1)}, bf16[1024]{0:T(1024)(128)(2,1)}, u32[]{:S(2)}) copy-start(bf16[1024]{0:T(1024)(128)(2,1)} %param.20) | copy-start | bytes 6148
  0.7 7.3 %copy-start.8 = (bf16[256]{0:T(256)(128)(2,1)S(1)}, bf16[256]{0:T(256)(128)(2,1)}, u32[]{:S(2)}) copy-start(bf16[256]{0:T(256)(128)(2,1)} %param.22) | copy-start | bytes 1540
  0.7 7.3 %copy-start.7 = (bf16[256]{0:T(256)(128)(2,1)S(1)}, bf16[256]{0:T(256)(128)(2,1)}, u32[]{:S(2)}) copy-start(bf16[256]{0:T(256)(128)(2,1)} %param.23) | copy-start | bytes 1540
  0.7 7.3 %copy-start.6 = (bf16[256]{0:T(256)(128)(2,1)S(1)}, bf16[256]{0:T(256)(128)(2,1)}, u32[]{:S(2)}) copy-start(bf16[256]{0:T(256)(128)(2,1)} %param.24) | copy-start | bytes 1540
  8.5 79.6 %copy-start.4 = (s32[512]{0:T(512)S(1)}, s32[512]{0:T(512)}, u32[]{:S(2)}) copy-start(s32[512]{0:T(512)} %param.14) | copy-start | bytes 6148
  263.5 2.8 %copy-start = (bf16[48,128,512]{2,1,0:T(8,128)(2,1)S(1)}, bf16[48,128,512]{2,1,0:T(8,128)(2,1)}, u32[]{:S(2)}) copy-start(bf16[48,128,512]{2,1,0:T(8,128)(2,1)} %get-tuple-element.38.in_ref) | copy-start | bytes 18874372
  266.3 5.1 %copy-start.3 = (f32[1,7168]{1,0:T(1,128)S(1)}, f32[1,7168]{1,0:T(1,128)}, u32[]{:S(2)}) copy-start(f32[1,7168]{1,0:T(1,128)} %get-tuple-element.42) | copy-start | bytes 86020
  266.3 6.3 %copy-start.2 = (bf16[512,1024]{1,0:T(8,128)(2,1)S(1)}, bf16[512,1024]{1,0:T(8,128)(2,1)}, u32[]{:S(2)}) copy-start(bf16[512,1024]{1,0:T(8,128)(2,1)} %get-tuple-element.62) | copy-start | bytes 3145732
  266.3 7.3 %copy-start.1 = (bf16[512,1024]{1,0:T(8,128)(2,1)S(1)}, bf16[512,1024]{1,0:T(8,128)(2,1)}, u32[]{:S(2)}) copy-start(bf16[512,1024]{1,0:T(8,128)(2,1)} %get-tuple-element.63) | copy-start | bytes 3145732

commit v2 on v1

v2 whole, which is shorter than its diff:
```python
import functools
from functools import partial
import math

import jax
import jax.numpy as jnp
from jax import lax
from jax.experimental import pallas as pl
from jax.experimental.pallas import tpu as pltpu
from jax.sharding import PartitionSpec as P

D = 1024
HEADS = 16
HEAD_DIM = 64
ROT_DIM = 32
TOK_DEV = 512

MESH = pl.DeviceIdType.MESH
BLK = 128
COL = 512
SLOTS = 8
LAGS = (1, 2, 2, 2, 2, 2, 2, 2)
TURN = 0
EARLY = 6

EPS = 1e-05
NEG = -1000000000.0
GELU_C = math.sqrt(2.0 / math.pi)
GELU_A = 0.044715
GATHER_LAGS = (0, 2, 4, 5)
SCORE_SCALE = 0.125


def spans_of(lengths_ref, owner_ref, device):
    mine = jnp.where(owner_ref[...] == device, lengths_ref[...], 0).astype(jnp.float32)
    even = lax.broadcasted_iota(jnp.int32, mine.shape, 1) % 2 == 0
    first = jnp.sum(jnp.where(even, mine, 0.0), axis=1, keepdims=True)
    return first.astype(jnp.int32), jnp.sum(mine, axis=1, keepdims=True).astype(jnp.int32)


GATHER_CHUNKS = (4, 4, 4, 1)
GATHER_PAIRS = (0, 6, 11, 12)
FBLK = 256


def front_steps(shards, small_ref, lengths_ref, owner_ref, tok_hbm, cot_hbm, owns, fulls,
                normed_ref, active_ref, gh_ref, up_ref, base_ref, gn_ref, tok_ref, gib_ref, norm_ref, small_full, bias_ref,
                send_sem, recv_sem, core_send, core_recv, own_send, own_recv, local_sem, s_send, s_recv):
    in_full, fc_full = fulls[:2]
    rep = lax.axis_index("rep")
    shard = lax.axis_index("shard")
    y, c = shard // 2, shard % 2
    b0, b1 = rep % 2, (rep // 2) % 2
    core_shard = 2 * y + 1 - c
    other = 2 * (1 - y) + c
    diagonal = 2 * (1 - y) + 1 - c
    core_peer = (rep, core_shard)
    y_peer = (rep, other)
    diagonal_peer = (rep, diagonal)
    peer0 = (rep + 1 - 2 * b0, shard)
    peer1 = (rep + 2 - 4 * b1, shard)
    group = (core_peer, y_peer, diagonal_peer)

    loads = [pltpu.make_async_copy(src, dst, local_sem.at[4 + j]) for j, (src, dst) in enumerate(((tok_hbm, tok_ref), (cot_hbm, up_ref)))]
    chunks = [(a, k) for a in range(4) for k in range(GATHER_CHUNKS[a])]
    n = len(chunks)
    ways = ((b0 + 2 * b1, b1, peer0, peer1), (b1 + 2 * b0, b0, peer1, peer0))

    def remote(src, dst, sems, index, peer):
        return pltpu.make_async_remote_copy(
            src_ref=src, dst_ref=dst, send_sem=sems[0].at[index], recv_sem=sems[1].at[index],
            device_id=peer, device_id_type=MESH)

    def place(i, h):
        a, k = chunks[i]
        own, full = owns[a], fulls[a]
        rows, cols = own.shape
        piece = rows // GATHER_CHUNKS[a] // 4
        return own, full, rows, k * 4 * piece, piece, pl.ds(h * (cols // 2), cols // 2)

    def held(i, h, piece):
        if i in GATHER_PAIRS:
            return (b0, b1)[h] * 2 * piece, 2 * piece
        return ways[h][0] * piece, piece

    def y_copy(i, h):
        own, full, rows, start, piece, cols = place(i, h)
        off, piece = held(i, h, piece)
        at = pl.multiple_of(start + off, 16)
        return remote(own.at[pl.ds(at, piece), cols],
                      full.at[pl.ds(pl.multiple_of(shard * rows + at, 16), piece), cols],
                      (send_sem, recv_sem), (0, i, h), y_peer)

    def first_copy(i, h):
        own, full, rows, start, piece, cols = place(i, h)
        off, piece = held(i, h, piece)
        at = pl.multiple_of(other * rows + start + off, 16)
        ref = full.at[pl.ds(at, piece), cols]
        return remote(ref, ref, (send_sem, recv_sem), (1, i, h), ways[h][2])

    def second_copy(i, h):
        own, full, rows, start, piece, cols = place(i, h)
        at = pl.multiple_of(other * rows + start + ways[h][1] * 2 * piece, 16)
        ref = full.at[pl.ds(at, 2 * piece), cols]
        return remote(ref, ref, (send_sem, recv_sem), (2, i, h), ways[h][3])

    def core_copy(i):
        own, full, rows, start, piece, cols = place(i, 0)
        ref = full.at[pl.ds(pl.multiple_of(other * rows + start, 16), 4 * piece)]
        return remote(ref, ref, (core_send, core_recv), (i,), core_peer)

    def own_rows(a):
        rows = owns[a].shape[0]
        return fulls[a].at[pl.ds(pl.multiple_of(shard * rows, 16), rows)]

    def own_copy(a):
        return remote(owns[a], own_rows(a), (own_send, own_recv), (a,), core_peer)

    def local_copy(a):
        return pltpu.make_async_copy(owns[a], own_rows(a), local_sem.at[a])

    def small_copy(j):
        return remote(small_ref, small_full.at[shard], (s_send, s_recv), (j,), group[j])

    def begin():
        for load in loads:
            load.start()
        for j in range(3):
            small_copy(j).start()
        for i in range(n):
            for h in range(2):
                y_copy(i, h).start()
        for a in range(4):
            own_copy(a).start()
            local_copy(a).start()

    def norm_all():
        small_full[shard] = small_ref[...]
        for j in range(3):
            small_copy(j).wait()
        for o in range(4):
            for r in range(8):
                bias_ref[0:1, (o * 8 + r) * 128:(o * 8 + r + 1) * 128] = small_full[o, r:r + 1, :]
            for r in range(2):
                span = slice((o * 2 + r) * 128, (o * 2 + r + 1) * 128)
                norm_ref[2:3, span] = small_full[o, 8 + r:9 + r, :]
                norm_ref[0:1, span] = small_full[o, 10 + r:11 + r, :]
                norm_ref[1:2, span] = small_full[o, 12 + r:13 + r, :]
        for load in loads:
            load.wait()

    def norm_rows(r, carry):
        at = pl.ds(pl.multiple_of(r * 64, 64), 64)
        x = tok_ref[at, :].astype(jnp.float32)
        center = x - jnp.mean(x, axis=-1, keepdims=True)
        spread = jnp.mean(center * center, axis=-1, keepdims=True)
        normed = center * lax.rsqrt(spread + EPS) * norm_ref[0:1, :] + norm_ref[1:2, :]
        normed_ref[at, :] = normed.astype(jnp.bfloat16)
        base_ref[at, :] = x + norm_ref[2:3, :]
        slot = lax.broadcasted_iota(jnp.int32, (64, 1), 0) + r * 64
        _, used = spans_of(lengths_ref, owner_ref, rep * shards + shard)
        up_ref[at, :] = jnp.where(slot < used, up_ref[at, :].astype(jnp.float32), 0.0).astype(jnp.bfloat16)
        return carry

    def span(j):
        return pl.ds(pl.multiple_of(j * FBLK, FBLK), FBLK)

    def hidden_block(j, carry):
        at = span(j)
        hidden = jnp.dot(normed_ref[...], in_full[:, at], preferred_element_type=jnp.float32) + bias_ref[0:1, at]
        cube = hidden * hidden
        turn = jnp.tanh(GELU_C * hidden * (1.0 + GELU_A * cube))
        half = 0.5 * (1.0 + turn)
        active_ref[:, at] = (hidden * half).astype(jnp.bfloat16)
        slope = half + 0.5 * hidden * (1.0 - turn * turn) * (GELU_C * (1.0 + 3.0 * GELU_A * cube))
        gh_ref[:, at] = slope.astype(jnp.bfloat16)
        return carry

    def back_block(j, carry):
        at = span(j)
        grad = lax.dot_general(up_ref[...], fc_full[at, :], (((1,), (1,)), ((), ())), preferred_element_type=jnp.float32)
        low = (grad * gh_ref[:, at].astype(jnp.float32)).astype(jnp.bfloat16)
        gh_ref[:, at] = low
        gib_ref[0:1, at] = jnp.sum(low.astype(jnp.float32), axis=0, keepdims=True)
        return carry

    def mlp_block(j, carry):
        at = span(j)
        base_ref[:, at] = base_ref[:, at] + jnp.dot(active_ref[...], fc_full[:, at], preferred_element_type=jnp.float32)
        return carry

    def grad_block(j, carry):
        at = span(j)
        gn_ref[:, at] = lax.dot_general(gh_ref[...], in_full[at, :], (((1,), (1,)), ((), ())), preferred_element_type=jnp.float32)
        return carry

    def loop(block, lo, hi):
        lax.fori_loop(lo, hi, block, 0)

    work = {1: [norm_all]}
    nf = 4096 // FBLK
    lag = GATHER_LAGS
    ends = [sum(GATHER_CHUNKS[:a + 1]) - 1 + lag[3] for a in range(4)]

    def ready(a):
        own_copy(a).wait_recv()
        local_copy(a).wait()

    def plan(step, *todo):
        work.setdefault(step, []).extend(todo)

    bind = functools.partial
    nd = D // FBLK
    for j in range(4):
        plan(1 + j, bind(loop, norm_rows, 2 * j, 2 * j + 2))
    plan(ends[0], bind(ready, 0))
    for j in range(4):
        plan(ends[0] + j, bind(loop, hidden_block, j * nf // 4, (j + 1) * nf // 4))
    plan(ends[1], bind(ready, 1))
    for j in range(2):
        plan(ends[1] + j, bind(loop, back_block, j * nf // 2, (j + 1) * nf // 2))
    for j in range(2):
        plan(ends[1] + 2 + j, bind(loop, grad_block, j * nd // 2, (j + 1) * nd // 2))
    for j in range(2):
        plan(ends[1] + 4 + j, bind(loop, mlp_block, j * nd // 2, (j + 1) * nd // 2))

    def step(i):
        if i < n:
            for h in range(2):
                y_copy(i, h).wait_recv()
                first_copy(i, h).start()
        if 0 <= i - lag[1] < n:
            for h in range(2):
                first_copy(i - lag[1], h).wait_recv()
                if i - lag[1] not in GATHER_PAIRS:
                    second_copy(i - lag[1], h).start()
            if i - lag[1] in GATHER_PAIRS:
                core_copy(i - lag[1]).start()
        if 0 <= i - lag[2] < n and i - lag[2] not in GATHER_PAIRS:
            for h in range(2):
                second_copy(i - lag[2], h).wait_recv()
            core_copy(i - lag[2]).start()
        if 0 <= i - lag[3] < n:
            core_copy(i - lag[3]).wait_recv()
        for todo in work.get(i, []):
            todo()

    def finish():
        ready(2)
        ready(3)
        for i in range(n):
            for h in range(2):
                y_copy(i, h).wait_send()
                first_copy(i, h).wait_send()
                if i not in GATHER_PAIRS:
                    second_copy(i, h).wait_send()
            core_copy(i).wait_send()
        for a in range(4):
            own_copy(a).wait_send()

    return begin, n + lag[3], ends[0] + 4, step, finish


QBLK = 256


def attend_pair(q, k, v, ga, bias_ref, cos_ref, sa_ref, sb_ref, put_att, put_grad):
    f32, bf = jnp.float32, jnp.bfloat16
    nt = (((1,), (1,)), ((), ()))
    tn = (((0,), (0,)), ((), ()))
    lane = lax.broadcasted_iota(jnp.int32, (1, 128), 1)
    keep = [(lane < HEAD_DIM).astype(f32).astype(bf), (lane >= HEAD_DIM).astype(f32).astype(bf)]
    q = q * jnp.asarray(SCORE_SCALE, bf)
    attended, grad_q = [], []
    grad_k, grad_v = {}, {}
    n_blocks = TOK_DEV // QBLK

    def add(store, block, value):
        store[block] = value if block not in store else store[block] + value

    for r in range(n_blocks):
        rows = slice(r * QBLK, (r + 1) * QBLK)
        keys = (r + 1) * QBLK
        att = gq = None
        for h in range(2):
            qh = q[rows] * keep[h]
            gh = ga[rows] * keep[h]
            kh = k[:keys] * keep[h]
            vh = v[:keys] * keep[h]
            scores = lax.dot_general(qh, k[:keys], nt, preferred_element_type=f32) + bias_ref[rows, :keys]
            weight = jnp.exp(scores - jnp.max(scores, axis=-1, keepdims=True))
            soft = weight * (1.0 / jnp.sum(weight, axis=-1, keepdims=True))
            low = soft.astype(bf)
            grad_soft = lax.dot_general(gh, v[:keys], nt, preferred_element_type=f32)
            weighted = soft * grad_soft
            delta = jnp.sum(weighted, axis=-1, keepdims=True)
            grad_scores = (weighted - soft * delta).astype(bf)
            part = jnp.dot(low, vh, preferred_element_type=f32)
            att = part if att is None else att + part
            part = jnp.dot(grad_scores, kh, preferred_element_type=f32)
            gq = part if gq is None else gq + part
            gk = lax.dot_general(grad_scores, qh, tn, preferred_element_type=f32)
            gv = lax.dot_general(low, gh, tn, preferred_element_type=f32)
            for b in range(r + 1):
                span = slice(b * QBLK, (b + 1) * QBLK)
                add(grad_k, b, gk[span])
                add(grad_v, b, gv[span])
        attended.append(att)
        grad_q.append(gq)

    def unturn(x):
        x = x.astype(bf).astype(f32)
        return x * cos_ref[...] - pltpu.roll(x, 127, 1) * sa_ref[...] - pltpu.roll(x, 1, 1) * sb_ref[...]

    put_att(jnp.concatenate(attended, 0).astype(bf))
    put_grad(0, unturn(jnp.concatenate(grad_q, 0) * SCORE_SCALE).astype(bf))
    put_grad(1, unturn(jnp.concatenate([grad_k[b] for b in range(n_blocks)], 0)).astype(bf))
    put_grad(2, jnp.concatenate([grad_v[b] for b in range(n_blocks)], 0).astype(bf))


def reduce_steps(n_rep, n_chunks, lengths_ref, owner_ref, pos_ref, norm_ref, out_hbm_blocks, small_out, layer_ref, grad_ref,
                 left, right, turned, qkv_full, out_full, gn_ref, base_ref, tok_ref, held_ref,
                 bias_ref, cos_ref, sa_ref, sb_ref, store_sem, c_send, c_keep, c_recv, acc, y_recv, recvs, s_buf, s_recv,
                 send_sem, recv_sem, s_send_sem, s_recv_sem):
    rep = lax.axis_index("rep")
    shard = lax.axis_index("shard")
    y, c = shard // 2, shard % 2
    nbits = int(math.log2(n_rep))
    bits = [(rep // (1 << b)) % 2 for b in range(nbits)]

    def rep_peer(b):
        return (rep + (1 << b) * (1 - 2 * bits[b]), shard)

    core_peer = (rep, shard + 1 - 2 * c)
    y_peer = (rep, shard + 2 - 4 * y)
    last = 3
    extra = list(range(last, nbits))
    half = BLK // 2

    def way(t):
        return (t % TURN) // (TURN - 1) if TURN else 0

    def pick(d, zero, one):
        return zero + d * (one - zero)

    def bit_of(k, d):
        return bits[2] if k == 2 else pick(d, bits[k], bits[1 - k])

    def bit_peer(k, d):
        return rep_peer(2) if k == 2 else (pick(d, rep_peer(k)[0], rep_peer(1 - k)[0]), shard)

    def base(k, d):
        off = 0
        for j in range(k):
            off = off + bit_of(j, d) * (half >> j)
        return off

    peers = [core_peer, y_peer] + [rep_peer(b) for b in range(nbits)]

    def copy(src, dst, stage, slot, peer):
        return pltpu.make_async_remote_copy(
            src_ref=src, dst_ref=dst, send_sem=send_sem.at[stage, slot],
            recv_sem=recv_sem.at[stage, slot], device_id=peer, device_id_type=MESH)

    def core_copy(t):
        s = t % SLOTS
        return copy(c_send.at[s], c_recv.at[s], 0, s, core_peer)

    def first_copy(t, d):
        s = t % SLOTS
        if d:
            return copy(acc.at[s, :, 1 - bits[1]], y_recv.at[s], 1, s, rep_peer(1))
        return copy(acc.at[s, 1 - y], y_recv.at[s], 1, s, y_peer)

    def second_copy(t):
        s, d = t % SLOTS, way(t)
        src = acc.at[s, pick(d, y, 1 - y), pick(d, 1 - bits[0], bits[1])]
        peer = (pick(d, rep_peer(0)[0], rep), pick(d, shard, y_peer[1]))
        return copy(src, recvs[0].at[s], 2, s, peer)

    def rows_copy(k, t):
        s, d = t % SLOTS, way(t)
        rows = half >> k
        start = pl.multiple_of(base(k + 1, d) - bit_of(0, d) * half + (1 - 2 * bit_of(k, d)) * rows, 16)
        return copy(acc.at[s, y, bit_of(0, d), pl.ds(start, rows)], recvs[k].at[s], 2 + k, s, bit_peer(k, d))

    def own(t):
        return pl.multiple_of(base(last, way(t)), 16)

    def own_acc(t, k=last):
        d = way(t)
        return t % SLOTS, y, bit_of(0, d), pl.ds(pl.multiple_of(base(k, d) - bit_of(0, d) * half, 16), half >> (k - 1))

    tail = BLK >> last

    def extra_copy(j, t):
        s = t % SLOTS
        return copy(acc.at[own_acc(t)], recvs[last + j].at[s], 2 + last + j, s, rep_peer(extra[j]))

    across = held_ref.shape[1] // COL

    def held(t, start, rows):
        at = pl.multiple_of(t // across * BLK + start, 16)
        return held_ref.at[pl.ds(at, rows), pl.ds(pl.multiple_of(t % across * COL, COL), COL)]

    def gather_copy(k, t):
        s, d = t % SLOTS, way(t)
        ref = held(t, base(k + 1, d), half >> k)
        return copy(ref, ref, 2 + last + len(extra) + k, s, bit_peer(k, d))

    f32, bf = jnp.float32, jnp.bfloat16
    nt = (((1,), (1,)), ((), ()))

    def block(start, j, size=256):
        return pl.ds(pl.multiple_of(start + j * size, size), size)

    def tables(u):
        first, used = spans_of(lengths_ref, owner_ref, rep * lax.axis_size("shard") + shard)
        lane = lax.broadcasted_iota(jnp.int32, (128, 128), 1)
        even = lane % 2 == 0
        lane = lane % HEAD_DIM
        inverse = jnp.exp((lane // 2).astype(f32) * (-2.0 * math.log(10000.0) / ROT_DIM))
        inverse = jnp.where(lane < ROT_DIM, inverse, 0.0)
        key = lax.broadcasted_iota(jnp.int32, (128, TOK_DEV), 1)
        for g in range(TOK_DEV // 128):
            rows = slice(g * 128, (g + 1) * 128)
            query = lax.broadcasted_iota(jnp.int32, (128, TOK_DEV), 0) + g * 128
            same = (query < used) & ((query < first) == (key < first))
            bias_ref[rows, :] = jnp.where((key == query) | ((key < query) & same), 0.0, NEG)
            place = jnp.broadcast_to(pos_ref[g:g + 1, :].astype(f32), (128, 128)).T
            angles = place * inverse
            sine = jnp.sin(angles)
            cos_ref[rows, :] = jnp.cos(angles)
            sa_ref[rows, :] = jnp.where(even, -sine, 0.0)
            sb_ref[rows, :] = jnp.where(even, 0.0, sine)

    def turn_rows(u):
        for b in range(2):
            rows = jnp.dot(left[:, 0:D], qkv_full[:, block(0, 2 * u + b)], preferred_element_type=f32)
            for g in range(2):
                part = rows[:, g * 128:(g + 1) * 128]
                part = part * cos_ref[...] + pltpu.roll(part, 127, 1) * sa_ref[...] + pltpu.roll(part, 1, 1) * sb_ref[...]
                right[:, block(0, 4 * u + 2 * b + g, 128)] = part.astype(bf)

    def value_rows(u):
        for b in range(2):
            at = block(2 * D, 2 * u + b)
            right[:, at] = jnp.dot(left[:, 0:D], qkv_full[:, at], preferred_element_type=f32).astype(bf)

    def grad_attended(u):
        for b in range(2):
            part = lax.dot_general(right[:, 3 * D:4 * D], out_full[block(0, 2 * u + b), :], nt, preferred_element_type=f32)
            left[:, block(D, 2 * u + b)] = part.astype(bf)

    def attend(u):
        @pl.when(u % 2 == 0)
        def _():
            pair = u // 2
            spans = [block(k * D, pair, 128) for k in range(3)]
            span = block(D, pair, 128)

            def put_att(value):
                left[:, span] = value

            def put_grad(part, value):
                right[:, spans[part]] = value
            attend_pair(right[:, spans[0]], right[:, spans[1]], right[:, spans[2]], left[:, span],
                        bias_ref, cos_ref, sa_ref, sb_ref, put_att, put_grad)

    def grad_normed(u):
        at = block(0, u)
        gn_ref[:, at] = gn_ref[:, at] + lax.dot_general(right[:, 0:3 * D], qkv_full[at, :], nt, preferred_element_type=f32)

    def project(u):
        for b in range(2):
            at = block(0, 2 * u + b)
            layer_ref[:, at] = (base_ref[:, at] + jnp.dot(left[:, D:2 * D], out_full[:, at], preferred_element_type=f32)).astype(bf)

    def norm_back(u):
        @pl.when(u == 0)
        def _():
            s_buf[0, :, 4 * D:] = jnp.zeros((1, 3 * D), f32)
        at = block(0, u, 64)
        x = tok_ref[at, :].astype(f32)
        center = x - jnp.mean(x, axis=-1, keepdims=True)
        scale = lax.rsqrt(jnp.mean(center * center, axis=-1, keepdims=True) + EPS)
        unit = center * scale
        grad = gn_ref[at, :]
        upstream = right[at, 3 * D:4 * D].astype(f32)
        wide = grad * norm_ref[0:1, :]
        lean = wide - jnp.mean(wide, axis=-1, keepdims=True) - unit * jnp.mean(wide * unit, axis=-1, keepdims=True)
        grad_ref[at, :] = (lean * scale + upstream).astype(bf)
        for k, value in enumerate((upstream, grad * unit, grad)):
            span = slice((4 + k) * D, (5 + k) * D)
            s_buf[0, :, span] = s_buf[0, :, span] + jnp.sum(value, axis=0, keepdims=True)

    tasks = [(6, 1, tables), (7, 4, turn_rows), (11, 2, value_rows), (13, 2, grad_attended), (15, 16, attend),
             (32, 4, grad_normed), (36, 2, project), (38, 8, norm_back)]

    def store(t):
        return pltpu.make_async_copy(held(t, 0, BLK), out_hbm_blocks.at[t], store_sem.at[t % 4])

    def compute(t):
        s = t % SLOTS
        first, stride, column, new = chunk_plan(t)

        @pl.when(new)
        def _():
            for o in range(4):
                at = pl.multiple_of(first + o * stride, BLK)
                turned[o % 2, (o // 2) * BLK:(o // 2 + 1) * BLK, :] = left[:, pl.ds(at, BLK)].T
        operand = right[:, pl.ds(pl.multiple_of(column, COL), COL)]
        for side, dst in ((1 - c, c_send), (c, c_keep)):
            part = jnp.dot(turned[side], operand, preferred_element_type=jnp.float32)
            dst[s] = part.astype(jnp.bfloat16).reshape(2, 2, half, COL)
        core_copy(t).start()

    def each_way(t, body):
        for d in range(2 if TURN else 1):
            @pl.when(way(t) == d)
            def _(d=d):
                body(d)

    def after_core(t):
        s = t % SLOTS
        core_copy(t).wait()

        def total(d):
            for own_half in range(2):
                if d:
                    at = (s, slice(None), bits[1] if own_half else 1 - bits[1])
                else:
                    at = (s, y if own_half else 1 - y)
                acc[at] = c_keep[at] + c_recv[at]
                if not own_half:
                    first_copy(t, d).start()
        each_way(t, total)

    def after_first(t):
        s = t % SLOTS

        def total(d):
            first_copy(t, d).wait()
            at = (s, slice(None), bits[1]) if d else (s, y)
            acc[at] = acc[at] + y_recv[s]
        each_way(t, total)
        second_copy(t).start()

    def after_rows(k, t):
        s = t % SLOTS
        (second_copy(t) if k == 0 else rows_copy(k, t)).wait()
        at = own_acc(t, k + 1)
        total = acc[at] + recvs[k][s]
        if k + 1 < last:
            acc[at] = total
            rows_copy(k + 1, t).start()
        elif extra:
            acc[at] = total
            extra_copy(0, t).start()
        else:
            held(t, base(last, way(t)), tail)[...] = total
            gather_copy(last - 1, t).start()

    def after_extra(j, t):
        s = t % SLOTS
        extra_copy(j, t).wait()
        total = acc[own_acc(t)] + recvs[last + j][s]
        if j + 1 < len(extra):
            acc[own_acc(t)] = total
            extra_copy(j + 1, t).start()
        else:
            held(t, base(last, way(t)), tail)[...] = total
            gather_copy(last - 1, t).start()

    def after_gather(k, t):
        gather_copy(k, t).wait()
        if k > 0:
            gather_copy(k - 1, t).start()
        else:
            @pl.when(t >= 4)
            def _():
                store(t - 4).wait()
            store(t).start()

    stages = [(0, compute), (LAGS[0], after_core), (LAGS[0]+LAGS[1], after_first)]
    lag = LAGS[0]+LAGS[1]
    for k in range(last):
        lag += LAGS[2+k]
        stages.append((lag, functools.partial(after_rows, k)))
    for j in range(len(extra)):
        lag += 1
        stages.append((lag, functools.partial(after_extra, j)))
    for k in reversed(range(last)):
        lag += LAGS[5+last-1-k]
        stages.append((lag, functools.partial(after_gather, k)))

    s_peers = peers

    def small_copy(j):
        return pltpu.make_async_remote_copy(
            src_ref=s_buf.at[j], dst_ref=s_recv.at[j], send_sem=s_send_sem.at[j],
            recv_sem=s_recv_sem.at[j], device_id=s_peers[j], device_id_type=MESH)

    def small_step(j):
        if j > 0:
            small_copy(j - 1).wait()
            total = s_buf[j - 1] + s_recv[j - 1]
            if j < len(s_peers):
                s_buf[j] = total
            else:
                small_out[...] = total
        if j < len(s_peers):
            small_copy(j).start()

    def step(i, carry):
        for delay, stage in reversed(stages):
            @pl.when((i >= delay) & (i < n_chunks + delay))
            def _(stage=stage, delay=delay):
                stage(i - delay)
        for start, count, task in tasks:
            @pl.when((i >= start) & (i < start + count))
            def _(start=start, task=task):
                task(i - start)
        for j in range(len(s_peers) + 1):
            @pl.when(i == 47 + j)
            def _(j=j):
                small_step(j)
        return carry

    def finish():
        for t in range(n_chunks - 4, n_chunks):
            store(t).wait()
    return n_chunks + lag, step, finish


def block_kernel(shards, n_rep, n_chunks, n_recvs, small_ref, lengths_ref, owner_ref, pos_ref, tok_hbm, cot_hbm,
                 in_own, fc_own, qkv_own, out_own, blocks_hbm, small_out, layer_ref, grad_ref,
                 in_full, fc_full, qkv_full, out_full, left, right, turned, gn_ref, base_ref, tok_ref,
                 small_full, ff_bias, norm_ref, bias_ref, cos_ref, sa_ref, sb_ref, s_buf, s_recv,
                 c_send, c_keep, c_recv, acc, y_recv, *rest):
    recvs, sems = rest[:n_recvs], rest[n_recvs:]
    rep = lax.axis_index("rep")
    shard = lax.axis_index("shard")
    barrier = pltpu.get_barrier_semaphore()
    peers = [(rep, 4 * (shard // 4) + (shard + k) % 4) for k in range(1, 4)]
    b = 1
    while b < n_rep:
        peers.append((rep + b * (1 - 2 * ((rep // b) % 2)), shard))
        b *= 2
    for p in peers:
        pl.semaphore_signal(barrier, inc=1, device_id=p, device_id_type=MESH)
    pl.semaphore_wait(barrier, len(peers))

    begin, gather_steps, free_from, gather_step, gather_finish = front_steps(
        shards, small_ref, lengths_ref, owner_ref, tok_hbm, cot_hbm,
        (in_own, fc_own, qkv_own, out_own), (in_full, fc_full, qkv_full, out_full),
        left.at[:, 0:D], left.at[:, 2 * D:6 * D], right.at[:, 4 * D:8 * D], right.at[:, 3 * D:4 * D],
        base_ref, gn_ref, tok_ref, s_buf.at[0], norm_ref, small_full, ff_bias, *sems[:9])
    total, step, finish = reduce_steps(
        n_rep, n_chunks, lengths_ref, owner_ref, pos_ref, norm_ref, blocks_hbm, small_out, layer_ref, grad_ref,
        left, right, turned, qkv_full, out_full, gn_ref, base_ref, tok_ref, in_full,
        bias_ref, cos_ref, sa_ref, sb_ref, sems[9], c_send, c_keep, c_recv, acc, y_recv, recvs, s_buf, s_recv, *sems[10:])
    begin()
    early = 0
    for i in range(gather_steps):
        gather_step(i)
        while i >= free_from and early < min(EARLY, (i - free_from + 1) * EARLY // (gather_steps - free_from)):
            step(early, 0)
            early += 1
    gather_finish()
    lax.fori_loop(early, total, step, 0)
    finish()


def block(small, lengths, owner, positions, tokens, cotangent, in_own, fc_own, qkv_own, out_own, n_rep, shards, n_chunks):
    nbits = int(math.log2(n_rep))
    last = 3
    n_extra = nbits - last
    n_stage = 2 + last + n_extra + last
    bf, f32 = jnp.bfloat16, jnp.float32
    rows = tokens.shape[0]
    ff = in_own.shape[1]
    n = sum(GATHER_CHUNKS)
    recv_rows = [BLK >> (k + 1) for k in range(last)] + [BLK >> last] * n_extra
    chunk = (SLOTS, 2, BLK // 2, COL)
    pair = (SLOTS, 2, 2, BLK // 2, COL)
    n_small = 2 + nbits
    sums = (1, 3 * D + ff)
    hbm = pl.BlockSpec(memory_space=pl.ANY)
    vm = pl.BlockSpec(memory_space=pltpu.VMEM)
    dma = pltpu.SemaphoreType.DMA

    def full(own):
        return pltpu.VMEM((own.shape[0] * shards, own.shape[1]), bf)
    return pl.pallas_call(
        functools.partial(block_kernel, shards, n_rep, n_chunks, len(recv_rows)),
        out_shape=(jax.ShapeDtypeStruct((n_chunks, BLK, COL), bf), jax.ShapeDtypeStruct(sums, f32),
                   jax.ShapeDtypeStruct((rows, D), bf), jax.ShapeDtypeStruct((rows, D), bf)),
        in_specs=[vm] * 4 + [hbm] * 6,
        out_specs=(hbm,) + (vm,) * 3,
        scratch_shapes=[
            full(in_own), full(fc_own), full(qkv_own), full(out_own),
            pltpu.VMEM((rows, 2 * D + ff), bf), pltpu.VMEM((rows, 4 * D + ff), bf), pltpu.VMEM((2, 2 * BLK, rows), bf),
            pltpu.VMEM((rows, D), f32), pltpu.VMEM((rows, D), f32), pltpu.VMEM((rows, D), bf),
            pltpu.VMEM((shards,) + small.shape, f32), pltpu.VMEM((1, ff), f32), pltpu.VMEM((8, D), f32),
            pltpu.VMEM((rows, rows), f32), *[pltpu.VMEM((rows, 128), f32)] * 3,
            pltpu.VMEM((n_small,) + sums, f32), pltpu.VMEM((n_small,) + sums, f32),
            pltpu.VMEM(pair, bf), pltpu.VMEM(pair, bf), pltpu.VMEM(pair, bf), pltpu.VMEM(pair, bf), pltpu.VMEM(chunk, bf),
            *[pltpu.VMEM((SLOTS, r, COL), bf) for r in recv_rows],
            dma((3, n, 2)), dma((3, n, 2)), dma((n,)), dma((n,)), dma((4,)), dma((4,)), dma((6,)), dma((3,)), dma((3,)),
            dma((4,)), dma((n_stage, SLOTS)), dma((n_stage, SLOTS)), dma((n_small,)), dma((n_small,)),
        ],
        compiler_params=pltpu.CompilerParams(collective_id=1, has_side_effects=True, vmem_limit_bytes=67043328),
        name="block",
    )(small, lengths, owner, positions, tokens, cotangent, in_own, fc_own, qkv_own, out_own)


def chunk_plan(t):
    cases = [
        (2 * D + (t // 2) * BLK, D, 3 * D + (t % 2) * COL, t % 2),
        (((t - 16) // 8) * BLK, D // 4, 4 * D + (t % 8) * COL, t % 8),
        (((t - 32) // 6) * BLK, D // 4, ((t - 32) % 6) * COL, (t - 32) % 6),
        (D + ((t - 44) // 2) * BLK, D // 4, 3 * D + (t % 2) * COL, t % 2),
    ]
    first, stride, column, within = (
        jnp.where(t < 16, cases[0][i], jnp.where(t < 32, cases[1][i], jnp.where(t < 44, cases[2][i], cases[3][i])))
        for i in range(4))
    return first, stride, column, within == 0


def assemble(blocks, places, scale):
    def kern(in_hbm, *rest):
        outs, (in_ref, stage, load_sem, sem) = rest[:-4], rest[-4:]
        copies = []
        part = 4

        def load(g):
            at = pl.ds(g * part, part)
            return pltpu.make_async_copy(in_hbm.at[at], in_ref.at[at], load_sem.at[g])
        for g in range(blocks.shape[0] // part):
            load(g).start()
        for (first, rows, cols), out in zip(places, outs):
            across = cols // COL
            for i in range(rows // BLK):
                for j in range(across):
                    t = first + i * across + j
                    if t % part == 0:
                        load(t // part).wait()
                    stage[t] = in_ref[t].astype(jnp.float32) * scale
                    copies.append(pltpu.make_async_copy(
                        stage.at[t], out.at[i * BLK:(i + 1) * BLK, j * COL:(j + 1) * COL], sem.at[t]))
                    copies[-1].start()
        for copy in copies:
            copy.wait()

    return pl.pallas_call(
        kern,
        out_shape=[jax.ShapeDtypeStruct((rows, cols), jnp.float32) for _, rows, cols in places],
        in_specs=[pl.BlockSpec(memory_space=pl.ANY)],
        out_specs=[pl.BlockSpec(memory_space=pl.ANY)] * len(places),
        scratch_shapes=[pltpu.VMEM(blocks.shape, blocks.dtype), pltpu.VMEM(blocks.shape, jnp.float32),
                        pltpu.SemaphoreType.DMA((blocks.shape[0] // 4,)), pltpu.SemaphoreType.DMA((blocks.shape[0],))],
        compiler_params=pltpu.CompilerParams(vmem_limit_bytes=63 * 2**20),
        name="assemble",
    )(blocks)


def body(
    tokens,
    positions,
    lengths,
    owner,
    qkv_weight,
    out_weight,
    in_weight,
    in_bias,
    fc_weight,
    fc_bias,
    norm_gain,
    norm_bias,
    cotangent,
):
    rep_count = lax.axis_size("rep")
    shard_count = lax.axis_size("shard")
    shard = lax.axis_index("shard")
    grad_scale = 1.0 / math.sqrt(TOK_DEV * rep_count * shard_count)
    lengths, owner = lengths.reshape(1, -1), owner.reshape(1, -1)
    small = sum(jnp.pad(part.astype(jnp.float32), (first, 2048 - first - part.shape[0])) for first, part in (
        (0, in_bias), (1024, fc_bias), (1280, norm_gain), (1536, norm_bias))).reshape(16, 128)
    blocks, small_sum, layer_out, input_grad = block(
        small, lengths, owner, positions.reshape(-1, 128), tokens, cotangent, in_weight, fc_weight, qkv_weight, out_weight,
        rep_count, shard_count, 48)
    small_sum = small_sum.reshape(-1) * grad_scale

    def own_part(first, size):
        return lax.dynamic_slice_in_dim(small_sum, first + shard * (size // 4), size // 4)

    grad_in, grad_fc, grad_qkv, grad_out = assemble(
        blocks, ((16, 256, 4 * D), (0, 1024, D), (32, 256, 3 * D), (44, 256, D)), grad_scale)
    return (
        layer_out,
        input_grad,
        grad_qkv,
        grad_out,
        grad_in,
        own_part(0, 4096),
        grad_fc,
        own_part(4096, D),
        own_part(4096 + D, D),
        own_part(4096 + 2 * D, D),
    )


def solution(mesh):
    in_specs = (
        P(("rep", "shard"), None),
        P(("rep", "shard")),
        P(),
        P(),
        P("shard", None),
        P("shard", None),
        P("shard", None),
        P("shard"),
        P("shard", None),
        P("shard"),
        P("shard"),
        P("shard"),
        P(("rep", "shard"), None),
    )
    out_specs = (
        P(("rep", "shard"), None),
        P(("rep", "shard"), None),
        P("shard", None),
        P("shard", None),
        P("shard", None),
        P("shard"),
        P("shard", None),
        P("shard"),
        P("shard"),
        P("shard"),
    )
    return jax.shard_map(body, mesh=mesh, in_specs=in_specs, out_specs=out_specs, check_vma=False)
```

time: 275 us -> 249 us (0.905)
  Pallas kernels: 258 us -> 240 us
  other arithmetic: 9.65 us -> 2.11 us
    pallas_call x2 -> x1, Pallas kernels: 253 us -> 233 us  [block(): pl.pallas_call(functools.partial(block_kernel, shards, n_rep, n_chunks, l...]
    select_n x4 -> x0, other arithmetic: 3.73 us -> none  [the longest x1 1.89 us: rotary_tables(): jnp.where(even, 0.0, sine)]
where the time goes in v2:
time: 249 us; the launch traced here: 248 us
  Pallas kernels  240 us (96%)
  local copies, waits for them, and re-layouts  5.7 us (2%)
    pallas_call x1, Pallas kernels, block(): pl.pallas_call(functools.partial(block_kernel, shards, n_rep, n_chunks, l...  233 us
    pallas_call x1, Pallas kernels, assemble(): pl.pallas_call(kern, out_shape=[jax.ShapeDtypeStruct((rows, cols), jnp.fl...  6.73 us

profile of v2, /device:TPU:0, one launch (start us, length us, event | category | flops | bytes accessed | tf_op | source)
XLA Modules:
  0.0 248.3 jit_solution(14951359205521304255)
XLA Ops:
  0.6 1.3 add_bitcast_fusion.small_ref
  2.0 233.1 %block.1 = (bf16[48,128,512]{2,1,0:T(8,128)(2,1)}, f32[1,7168]{1,0:T(1,128)}, bf16[512,1024]{1,0:T(8,128)(2,1)}, bf16[512,1024]{1,0:T(8,128)(2,1)}) custom-call(f32[16,128]{1,0:T(8,128)} %add_bitcast_fusion.small_ref, s32[1,64]{1,0:T(1,128)} %bitcast.14, s32[1,64]{1,0:T(1,128)} %bitcast.15, s32[4,128]{1,0:T(4,128)} %bitcast.10, bf16[512,1024]{1,0:T(8,128)(2,1)} %tok_hbm.1, ...), custom_call_target="tpu_custom_call" | custom-call | tf_op jit(solution)/shard_map/block/pallas_call | solution.py:695
  235.1 0.8 broadcast_multiply_fusion
  235.9 0.6 constant_dynamic-slice_fusion
  236.4 0.6 constant_dynamic-slice_fusion.3
  237.0 6.7 %assemble.1 = (f32[256,4096]{1,0:T(8,128)}, f32[1024,1024]{1,0:T(8,128)}, f32[256,3072]{1,0:T(8,128)}, f32[256,1024]{1,0:T(8,128)}) custom-call(bf16[48,128,512]{2,1,0:T(8,128)(2,1)} %get-tuple-element.20.in_hbm), custom_call_target="tpu_custom_call" | custom-call | tf_op jit(solution)/shard_map/assemble/pallas_call | solution.py:756
  243.8 2.3 copy.25
  246.0 2.3 copy.26

commit v3 on v2

--- a/solution.py
+++ b/solution.py
@@ -21,7 +21,8 @@
 SLOTS = 8
 LAGS = (1, 2, 2, 2, 2, 2, 2, 2)
 TURN = 0
-EARLY = 6
+WRITES = 7
+EARLY = 10
 
 EPS = 1e-05
 NEG = -1000000000.0
@@ -39,7 +40,7 @@
 
 
 GATHER_CHUNKS = (4, 4, 4, 1)
-GATHER_PAIRS = (0, 6, 11, 12)
+GATHER_PAIRS = (4, 6, 11, 12)
 FBLK = 256
 
 
@@ -166,7 +167,7 @@
         return pl.ds(pl.multiple_of(j * FBLK, FBLK), FBLK)
 
     def hidden_block(j, carry):
-        at = span(j)
+        at = span(j % 4 * (4096 // FBLK // 4) + j // 4)
         hidden = jnp.dot(normed_ref[...], in_full[:, at], preferred_element_type=jnp.float32) + bias_ref[0:1, at]
         cube = hidden * hidden
         turn = jnp.tanh(GELU_C * hidden * (1.0 + GELU_A * cube))
@@ -245,20 +246,26 @@
         for todo in work.get(i, []):
             todo()
 
+    def sent(a):
+        for i in range(n):
+            if chunks[i][0] == a:
+                for h in range(2):
+                    y_copy(i, h).wait_send()
+                    first_copy(i, h).wait_send()
+                    if i not in GATHER_PAIRS:
+                        second_copy(i, h).wait_send()
+                core_copy(i).wait_send()
+        own_copy(a).wait_send()
+
+    plan(ends[1] + 3, bind(sent, 0))
+
     def finish():
         ready(2)
         ready(3)
-        for i in range(n):
-            for h in range(2):
-                y_copy(i, h).wait_send()
-                first_copy(i, h).wait_send()
-                if i not in GATHER_PAIRS:
-                    second_copy(i, h).wait_send()
-            core_copy(i).wait_send()
-        for a in range(4):
-            own_copy(a).wait_send()
-
-    return begin, n + lag[3], ends[0] + 4, step, finish
+        for a in range(1, 4):
+            sent(a)
+
+    return begin, n + lag[3], ends[0], ends[1] + 3, step, finish
 
 
 QBLK = 256
@@ -318,8 +325,8 @@
     put_grad(2, jnp.concatenate([grad_v[b] for b in range(n_blocks)], 0).astype(bf))
 
 
-def reduce_steps(n_rep, n_chunks, lengths_ref, owner_ref, pos_ref, norm_ref, out_hbm_blocks, small_out, layer_ref, grad_ref,
-                 left, right, turned, qkv_full, out_full, gn_ref, base_ref, tok_ref, held_ref,
+def reduce_steps(n_rep, n_chunks, lengths_ref, owner_ref, pos_ref, norm_ref, out_hbm_blocks, small_out, layer_hbm, grad_hbm,
+                 layer_ref, grad_ref, left, right, turned, qkv_full, out_full, gn_ref, base_ref, tok_ref, held_ref,
                  bias_ref, cos_ref, sa_ref, sb_ref, store_sem, c_send, c_keep, c_recv, acc, y_recv, recvs, s_buf, s_recv,
                  send_sem, recv_sem, s_send_sem, s_recv_sem):
     rep = lax.axis_index("rep")
@@ -494,8 +501,16 @@
             span = slice((4 + k) * D, (5 + k) * D)
             s_buf[0, :, span] = s_buf[0, :, span] + jnp.sum(value, axis=0, keepdims=True)
 
-    tasks = [(6, 1, tables), (7, 4, turn_rows), (11, 2, value_rows), (13, 2, grad_attended), (15, 16, attend),
-             (32, 4, grad_normed), (36, 2, project), (38, 8, norm_back)]
+    row_copies = [pltpu.make_async_copy(src, dst, store_sem.at[4 + j])
+                  for j, (src, dst) in enumerate(((layer_ref, layer_hbm), (grad_ref, grad_hbm)))]
+
+    def send_rows(u):
+        for row_copy in row_copies:
+            row_copy.start()
+
+    tasks = [(0, 1, tables), (EARLY, 4, turn_rows), (EARLY, 2, value_rows), (EARLY + 2, 2, grad_attended),
+             (EARLY + 4, 16, attend), (EARLY + 20, 4, grad_normed), (EARLY + 24, 2, project), (EARLY + 26, 8, norm_back),
+             (EARLY + 34, 1, send_rows)]
 
     def store(t):
         return pltpu.make_async_copy(held(t, 0, BLK), out_hbm_blocks.at[t], store_sem.at[t % 4])
@@ -630,14 +645,16 @@
     def finish():
         for t in range(n_chunks - 4, n_chunks):
             store(t).wait()
+        for row_copy in row_copies:
+            row_copy.wait()
     return n_chunks + lag, step, finish
 
 
 def block_kernel(shards, n_rep, n_chunks, n_recvs, small_ref, lengths_ref, owner_ref, pos_ref, tok_hbm, cot_hbm,
-                 in_own, fc_own, qkv_own, out_own, blocks_hbm, small_out, layer_ref, grad_ref,
+                 in_own, fc_own, qkv_own, out_own, blocks_hbm, small_out, layer_hbm, grad_hbm,
                  in_full, fc_full, qkv_full, out_full, left, right, turned, gn_ref, base_ref, tok_ref,
                  small_full, ff_bias, norm_ref, bias_ref, cos_ref, sa_ref, sb_ref, s_buf, s_recv,
-                 c_send, c_keep, c_recv, acc, y_recv, *rest):
+                 layer_ref, grad_ref, c_send, c_keep, c_recv, acc, y_recv, *rest):
     recvs, sems = rest[:n_recvs], rest[n_recvs:]
     rep = lax.axis_index("rep")
     shard = lax.axis_index("shard")
@@ -651,20 +668,21 @@
         pl.semaphore_signal(barrier, inc=1, device_id=p, device_id_type=MESH)
     pl.semaphore_wait(barrier, len(peers))
 
-    begin, gather_steps, free_from, gather_step, gather_finish = front_steps(
+    begin, gather_steps, free_from, in_done, gather_step, gather_finish = front_steps(
         shards, small_ref, lengths_ref, owner_ref, tok_hbm, cot_hbm,
         (in_own, fc_own, qkv_own, out_own), (in_full, fc_full, qkv_full, out_full),
         left.at[:, 0:D], left.at[:, 2 * D:6 * D], right.at[:, 4 * D:8 * D], right.at[:, 3 * D:4 * D],
         base_ref, gn_ref, tok_ref, s_buf.at[0], norm_ref, small_full, ff_bias, *sems[:9])
     total, step, finish = reduce_steps(
-        n_rep, n_chunks, lengths_ref, owner_ref, pos_ref, norm_ref, blocks_hbm, small_out, layer_ref, grad_ref,
-        left, right, turned, qkv_full, out_full, gn_ref, base_ref, tok_ref, in_full,
+        n_rep, n_chunks, lengths_ref, owner_ref, pos_ref, norm_ref, blocks_hbm, small_out, layer_hbm, grad_hbm,
+        layer_ref, grad_ref, left, right, turned, qkv_full, out_full, gn_ref, base_ref, tok_ref, in_full,
         bias_ref, cos_ref, sa_ref, sb_ref, sems[9], c_send, c_keep, c_recv, acc, y_recv, recvs, s_buf, s_recv, *sems[10:])
     begin()
     early = 0
     for i in range(gather_steps):
         gather_step(i)
-        while i >= free_from and early < min(EARLY, (i - free_from + 1) * EARLY // (gather_steps - free_from)):
+        due = (i - free_from + 1) * EARLY // (gather_steps - free_from)
+        while early < (due if i >= in_done else min(due, WRITES)):
             step(early, 0)
             early += 1
     gather_finish()
@@ -697,7 +715,7 @@
         out_shape=(jax.ShapeDtypeStruct((n_chunks, BLK, COL), bf), jax.ShapeDtypeStruct(sums, f32),
                    jax.ShapeDtypeStruct((rows, D), bf), jax.ShapeDtypeStruct((rows, D), bf)),
         in_specs=[vm] * 4 + [hbm] * 6,
-        out_specs=(hbm,) + (vm,) * 3,
+        out_specs=(hbm, vm, hbm, hbm),
         scratch_shapes=[
             full(in_own), full(fc_own), full(qkv_own), full(out_own),
             pltpu.VMEM((rows, 2 * D + ff), bf), pltpu.VMEM((rows, 4 * D + ff), bf), pltpu.VMEM((2, 2 * BLK, rows), bf),
@@ -705,10 +723,11 @@
             pltpu.VMEM((shards,) + small.shape, f32), pltpu.VMEM((1, ff), f32), pltpu.VMEM((8, D), f32),
             pltpu.VMEM((rows, rows), f32), *[pltpu.VMEM((rows, 128), f32)] * 3,
             pltpu.VMEM((n_small,) + sums, f32), pltpu.VMEM((n_small,) + sums, f32),
+            pltpu.VMEM((rows, D), bf), pltpu.VMEM((rows, D), bf),
             pltpu.VMEM(pair, bf), pltpu.VMEM(pair, bf), pltpu.VMEM(pair, bf), pltpu.VMEM(pair, bf), pltpu.VMEM(chunk, bf),
             *[pltpu.VMEM((SLOTS, r, COL), bf) for r in recv_rows],
             dma((3, n, 2)), dma((3, n, 2)), dma((n,)), dma((n,)), dma((4,)), dma((4,)), dma((6,)), dma((3,)), dma((3,)),
-            dma((4,)), dma((n_stage, SLOTS)), dma((n_stage, SLOTS)), dma((n_small,)), dma((n_small,)),
+            dma((6,)), dma((n_stage, SLOTS)), dma((n_stage, SLOTS)), dma((n_small,)), dma((n_small,)),
         ],
         compiler_params=pltpu.CompilerParams(collective_id=1, has_side_effects=True, vmem_limit_bytes=67043328),
         name="block",
@@ -728,10 +747,17 @@
     return first, stride, column, within == 0
 
 
-def assemble(blocks, places, scale):
+def assemble(blocks, rows, places, scale):
     def kern(in_hbm, *rest):
-        outs, (in_ref, stage, load_sem, sem) = rest[:-4], rest[-4:]
+        n = len(rows)
+        row_hbm, row_out, row_ref, outs = rest[:n], rest[n:2 * n], rest[-4 - n:-4], rest[2 * n:-4 - n]
+        in_ref, stage, load_sem, sem = rest[-4:]
+        first_row = blocks.shape[0]
         copies = []
+        row_loads = [pltpu.make_async_copy(row_hbm[j], row_ref[j], sem.at[first_row + j]) for j in range(n)]
+        row_stores = [pltpu.make_async_copy(row_ref[j], row_out[j], sem.at[first_row + n + j]) for j in range(n)]
+        for load_row in row_loads:
+            load_row.start()
         part = 4
 
         def load(g):
@@ -739,9 +765,13 @@
             return pltpu.make_async_copy(in_hbm.at[at], in_ref.at[at], load_sem.at[g])
         for g in range(blocks.shape[0] // part):
             load(g).start()
-        for (first, rows, cols), out in zip(places, outs):
+        for load_row, store_row in zip(row_loads, row_stores):
+            load_row.wait()
+            store_row.start()
+            copies.append(store_row)
+        for (first, height, cols), out in zip(places, outs):
             across = cols // COL
-            for i in range(rows // BLK):
+            for i in range(height // BLK):
                 for j in range(across):
                     t = first + i * across + j
                     if t % part == 0:
@@ -755,14 +785,15 @@
 
     return pl.pallas_call(
         kern,
-        out_shape=[jax.ShapeDtypeStruct((rows, cols), jnp.float32) for _, rows, cols in places],
-        in_specs=[pl.BlockSpec(memory_space=pl.ANY)],
-        out_specs=[pl.BlockSpec(memory_space=pl.ANY)] * len(places),
-        scratch_shapes=[pltpu.VMEM(blocks.shape, blocks.dtype), pltpu.VMEM(blocks.shape, jnp.float32),
-                        pltpu.SemaphoreType.DMA((blocks.shape[0] // 4,)), pltpu.SemaphoreType.DMA((blocks.shape[0],))],
+        out_shape=[jax.ShapeDtypeStruct(x.shape, x.dtype) for x in rows]
+        + [jax.ShapeDtypeStruct((height, cols), jnp.float32) for _, height, cols in places],
+        in_specs=[pl.BlockSpec(memory_space=pl.ANY)] * (1 + len(rows)),
+        out_specs=[pl.BlockSpec(memory_space=pl.ANY)] * (len(rows) + len(places)),
+        scratch_shapes=[*[pltpu.VMEM(x.shape, x.dtype) for x in rows], pltpu.VMEM(blocks.shape, blocks.dtype), pltpu.VMEM(blocks.shape, jnp.float32),
+                        pltpu.SemaphoreType.DMA((blocks.shape[0] // 4,)), pltpu.SemaphoreType.DMA((blocks.shape[0] + 2 * len(rows),))],
         compiler_params=pltpu.CompilerParams(vmem_limit_bytes=63 * 2**20),
         name="assemble",
-    )(blocks)
+    )(blocks, *rows)
 
 
 def body(
@@ -795,8 +826,8 @@
     def own_part(first, size):
         return lax.dynamic_slice_in_dim(small_sum, first + shard * (size // 4), size // 4)
 
-    grad_in, grad_fc, grad_qkv, grad_out = assemble(
-        blocks, ((16, 256, 4 * D), (0, 1024, D), (32, 256, 3 * D), (44, 256, D)), grad_scale)
+    layer_out, input_grad, grad_in, grad_fc, grad_qkv, grad_out = assemble(
+        blocks, (layer_out, input_grad), ((16, 256, 4 * D), (0, 1024, D), (32, 256, 3 * D), (44, 256, D)), grad_scale)
     return (
         layer_out,
         input_grad,

time: 249 us -> 235 us (0.944)
  Pallas kernels: 240 us -> 231 us
  local copies, waits for them, and re-layouts: 5.7 us -> 1.18 us
    pallas_call x1, Pallas kernels: 233 us -> 222 us  [block(): pl.pallas_call(functools.partial(block_kernel, shards, n_rep, n_chunks, l...]
    unnamed x2 -> x0, local copies, waits for them, and re-layouts: 4.52 us -> none
where the time goes in v3:
time: 235 us
  Pallas kernels  231 us (98%)
    pallas_call x1, Pallas kernels, block(): pl.pallas_call(functools.partial(block_kernel, shards, n_rep, n_chunks, l...  222 us
    pallas_call x1, Pallas kernels, assemble(): pl.pallas_call(kern, out_shape=[jax.ShapeDtypeStruct(x.shape, x.dtype) fo...  8.62 us

profile of v3, /device:TPU:0, one launch (start us, length us, event | category | flops | bytes accessed | tf_op | source)
XLA Modules:
  0.0 234.7 jit_solution(8987652286123396476)
XLA Ops:
  0.6 1.3 add_bitcast_fusion.small_ref
  2.0 222.0 %block.1 = (bf16[48,128,512]{2,1,0:T(8,128)(2,1)}, f32[1,7168]{1,0:T(1,128)}, bf16[512,1024]{1,0:T(8,128)(2,1)}, bf16[512,1024]{1,0:T(8,128)(2,1)}) custom-call(f32[16,128]{1,0:T(8,128)} %add_bitcast_fusion.small_ref, s32[1,64]{1,0:T(1,128)} %bitcast.14, s32[1,64]{1,0:T(1,128)} %bitcast.15, s32[4,128]{1,0:T(4,128)} %bitcast.10, bf16[512,1024]{1,0:T(8,128)(2,1)} %tok_hbm.1, ...), custom_call_target="tpu_custom_call" | custom-call | tf_op jit(solution)/shard_map/block/pallas_call | solution.py:713
  224.0 0.8 broadcast_multiply_fusion
  224.8 0.6 constant_dynamic-slice_fusion
  225.4 0.6 constant_dynamic-slice_fusion.3
  226.0 8.6 %assemble.1 = (bf16[512,1024]{1,0:T(8,128)(2,1)}, bf16[512,1024]{1,0:T(8,128)(2,1)}, f32[256,4096]{1,0:T(8,128)}, f32[1024,1024]{1,0:T(8,128)}, f32[256,3072]{1,0:T(8,128)}, /*index=5*/f32[256,1024]{1,0:T(8,128)}) custom-call(bf16[48,128,512]{2,1,0:T(8,128)(2,1)} %get-tuple-element.20.in_hbm, bf16[512,1024]{1,0:T(8,128)(2,1)} %get-tuple-element.21.rest_0_, ...), custom_call_target="tpu_custom_call" | custom-call | tf_op jit(solution)/shard_map/assemble/pallas_call | solution.py:786

commit v4 on v3

--- a/solution.py
+++ b/solution.py
@@ -185,11 +185,6 @@
         gib_ref[0:1, at] = jnp.sum(low.astype(jnp.float32), axis=0, keepdims=True)
         return carry
 
-    def mlp_block(j, carry):
-        at = span(j)
-        base_ref[:, at] = base_ref[:, at] + jnp.dot(active_ref[...], fc_full[:, at], preferred_element_type=jnp.float32)
-        return carry
-
     def grad_block(j, carry):
         at = span(j)
         gn_ref[:, at] = lax.dot_general(gh_ref[...], in_full[at, :], (((1,), (1,)), ((), ())), preferred_element_type=jnp.float32)
@@ -222,8 +217,6 @@
         plan(ends[1] + j, bind(loop, back_block, j * nf // 2, (j + 1) * nf // 2))
     for j in range(2):
         plan(ends[1] + 2 + j, bind(loop, grad_block, j * nd // 2, (j + 1) * nd // 2))
-    for j in range(2):
-        plan(ends[1] + 4 + j, bind(loop, mlp_block, j * nd // 2, (j + 1) * nd // 2))
 
     def step(i):
         if i < n:
@@ -326,7 +319,7 @@
 
 
 def reduce_steps(n_rep, n_chunks, lengths_ref, owner_ref, pos_ref, norm_ref, out_hbm_blocks, small_out, layer_hbm, grad_hbm,
-                 layer_ref, grad_ref, left, right, turned, qkv_full, out_full, gn_ref, base_ref, tok_ref, held_ref,
+                 layer_ref, grad_ref, left, right, turned, fc_full, qkv_full, out_full, gn_ref, base_ref, tok_ref, held_ref,
                  bias_ref, cos_ref, sa_ref, sb_ref, store_sem, c_send, c_keep, c_recv, acc, y_recv, recvs, s_buf, s_recv,
                  send_sem, recv_sem, s_send_sem, s_recv_sem):
     rep = lax.axis_index("rep")
@@ -478,6 +471,10 @@
         at = block(0, u)
         gn_ref[:, at] = gn_ref[:, at] + lax.dot_general(right[:, 0:3 * D], qkv_full[at, :], nt, preferred_element_type=f32)
 
+    def feed_forward(u):
+        at = block(0, u)
+        base_ref[:, at] = base_ref[:, at] + jnp.dot(left[:, 2 * D:6 * D], fc_full[:, at], preferred_element_type=f32)
+
     def project(u):
         for b in range(2):
             at = block(0, 2 * u + b)
@@ -509,8 +506,8 @@
             row_copy.start()
 
     tasks = [(0, 1, tables), (EARLY, 4, turn_rows), (EARLY, 2, value_rows), (EARLY + 2, 2, grad_attended),
-             (EARLY + 4, 16, attend), (EARLY + 20, 4, grad_normed), (EARLY + 24, 2, project), (EARLY + 26, 8, norm_back),
-             (EARLY + 34, 1, send_rows)]
+             (EARLY + 4, 16, attend), (EARLY + 20, 4, grad_normed), (EARLY + 24, 4, feed_forward), (EARLY + 28, 2, project),
+             (EARLY + 28, 8, norm_back), (EARLY + 36, 1, send_rows)]
 
     def store(t):
         return pltpu.make_async_copy(held(t, 0, BLK), out_hbm_blocks.at[t], store_sem.at[t % 4])
@@ -675,7 +672,7 @@
         base_ref, gn_ref, tok_ref, s_buf.at[0], norm_ref, small_full, ff_bias, *sems[:9])
     total, step, finish = reduce_steps(
         n_rep, n_chunks, lengths_ref, owner_ref, pos_ref, norm_ref, blocks_hbm, small_out, layer_hbm, grad_hbm,
-        layer_ref, grad_ref, left, right, turned, qkv_full, out_full, gn_ref, base_ref, tok_ref, in_full,
+        layer_ref, grad_ref, left, right, turned, fc_full, qkv_full, out_full, gn_ref, base_ref, tok_ref, in_full,
         bias_ref, cos_ref, sa_ref, sb_ref, sems[9], c_send, c_keep, c_recv, acc, y_recv, recvs, s_buf, s_recv, *sems[10:])
     begin()
     early = 0

time: 235 us -> 234 us (level)
  no operation moved by 1% of the time
where the time goes in v4:
time: 234 us
  Pallas kernels  229 us (98%)
    pallas_call x1, Pallas kernels, block(): pl.pallas_call(functools.partial(block_kernel, shards, n_rep, n_chunks, l...  221 us
    pallas_call x1, Pallas kernels, assemble(): pl.pallas_call(kern, out_shape=[jax.ShapeDtypeStruct(x.shape, x.dtype) fo...  8.62 us

profile of v4, /device:TPU:0, one launch (start us, length us, event | category | flops | bytes accessed | tf_op | source)
XLA Modules:
  0.0 233.6 jit_solution(3876291464823893022)
XLA Ops:
  0.6 1.3 add_bitcast_fusion.small_ref
  2.0 220.8 %block.1 = (bf16[48,128,512]{2,1,0:T(8,128)(2,1)}, f32[1,7168]{1,0:T(1,128)}, bf16[512,1024]{1,0:T(8,128)(2,1)}, bf16[512,1024]{1,0:T(8,128)(2,1)}) custom-call(f32[16,128]{1,0:T(8,128)} %add_bitcast_fusion.small_ref, s32[1,64]{1,0:T(1,128)} %bitcast.14, s32[1,64]{1,0:T(1,128)} %bitcast.15, s32[4,128]{1,0:T(4,128)} %bitcast.10, bf16[512,1024]{1,0:T(8,128)(2,1)} %tok_hbm.1, ...), custom_call_target="tpu_custom_call" | custom-call | tf_op jit(solution)/shard_map/block/pallas_call | solution.py:710
  222.8 0.8 broadcast_multiply_fusion
  223.6 0.6 constant_dynamic-slice_fusion
  224.2 0.6 constant_dynamic-slice_fusion.3
  224.8 8.6 %assemble.1 = (bf16[512,1024]{1,0:T(8,128)(2,1)}, bf16[512,1024]{1,0:T(8,128)(2,1)}, f32[256,4096]{1,0:T(8,128)}, f32[1024,1024]{1,0:T(8,128)}, f32[256,3072]{1,0:T(8,128)}, /*index=5*/f32[256,1024]{1,0:T(8,128)}) custom-call(bf16[48,128,512]{2,1,0:T(8,128)(2,1)} %get-tuple-element.20.in_hbm, bf16[512,1024]{1,0:T(8,128)(2,1)} %get-tuple-element.21.rest_0_, ...), custom_call_target="tpu_custom_call" | custom-call | tf_op jit(solution)/shard_map/assemble/pallas_call | solution.py:783
